TPU v7x, 256 devices: a whole 4x4x8 slice. The times are simulated.
256 devices in a mesh: lon: 64 (over y_lo, z, x), lat: 4 (over y_hi, core).
Axes of the slice: x: 4, y: 4 (y_hi: 2, y_lo: 2; y = y_hi * 2 + y_lo), z: 8, core: 2. Of those that a mesh axis runs over, the one named last changes fastest.
Arguments:
- observed: float32 [2, 4096, 1024], P(None, 'lon', 'lat')
- kappa_squared: float32 [2, 4096, 1024], P(None, 'lon', 'lat'), may hold values from 0.05 to 4
- probe_bits: int32 [2, 2, 4096, 1024], P(None, None, 'lon', 'lat'), may hold values from 0 to 255
- land_sea: int32 [4096, 1024], P('lon', 'lat'), may hold values from 0 to 1, as said below
- coarse_block_inverse: float32 [2, 32, 2, 32], replicated, as said below
Outputs:
- solution: float32 [2, 4096, 1024], P(None, 'lon', 'lat')
- diagonal_estimate: float32 [2, 4096, 1024], P(None, 'lon', 'lat')
- holdout_residual: float32 [2, 4096, 1024], P(None, 'lon', 'lat')
Inputs may be any that keep to these rules, and one draw needn't show every extreme that they name: `land_sea`: 1 marks an ocean cell, 0 land. `coarse_block_inverse`: symmetric and positive definite as a matrix of 64 rows.
All inputs are finite; a program needn't handle non-finite values.
Results may differ from a plain program's by a relative error of at most 0.0003.
Values sent between devices are 32-bit elements; how exact they have to be, the bound alone decides.
No kernel may reach another device: no remote copies, remote signals or barrier semaphores. Data moves between devices by JAX's collectives and lax.ppermute only.
A program may use at most 128 MiB of HBM per device.

v0:
```python
import functools

import jax
import jax.numpy as jnp
from jax import lax
from jax.experimental import pallas as pl
from jax.experimental.pallas import tpu as pltpu
from jax.sharding import PartitionSpec as P

BLK = 32
PROBES = 16
HALO = 3
TOP = 8
LANES = 128
EXACT = lax.Precision.HIGHEST
F32 = jnp.float32


def vmem(count):
    return [pl.BlockSpec(memory_space=pltpu.VMEM)] * count


def shape(*dims):
    return jax.ShapeDtypeStruct(dims, F32)


def iota(dims, axis):
    return lax.broadcasted_iota(jnp.int32, dims, axis)


def same_row(ref, row, stride):
    found = []
    for tile in range(ref.shape[0]):
        if stride == 0:
            found.append(jnp.broadcast_to(ref[tile, pl.ds(row, 1), :], (8, LANES)))
        else:
            found.append(ref[tile, pl.ds(row, 8, stride=stride), :])
    return jnp.concatenate(found, axis=1)


def keep(ref, value):
    for tile in range(ref.shape[0]):
        ref[tile] = value[:, tile * LANES : tile * LANES + LANES]


def row_of(ref, row):
    return jnp.broadcast_to(ref[pl.ds(row, 1), :], (8, ref.shape[1]))


def block_lanes(lat_at, level, width):
    source = iota((width, LANES), 0)
    lane = iota((width, LANES), 1)
    return jnp.where(lane == 64 + 16 * lat_at + 8 * level + source // BLK, 1.0, 0.0).astype(F32)


def block_sums(lat_at, rows):
    total = None
    for level in range(2):
        part = jnp.dot(
            rows[level],
            block_lanes(lat_at, level, rows[level].shape[1]),
            precision=EXACT,
            preferred_element_type=F32,
        )
        total = part if total is None else total + part
    return total


def first_row(row):
    return jnp.where(iota((8, row.shape[1]), 0) == 0, jnp.broadcast_to(row, (8, row.shape[1])), 0.0)


def raw_fields(obs, kap, bits, land):
    return (
        [obs[level] for level in range(2)]
        + [kap[level] for level in range(2)]
        + [bits[word, level].astype(F32) for word in range(2) for level in range(2)]
        + [land[...].astype(F32)]
    )


def prepare_kernel(obs, kap, bits, land, to_prev, to_next, own, ocean):
    lat_at = lax.axis_index("lat")
    lon_rows, width = land.shape
    fields = raw_fields(obs, kap, bits, land)
    lane = iota((lon_rows, LANES), 1)
    edges = jnp.zeros((lon_rows, LANES), F32)
    to_prev[...] = jnp.zeros(to_prev.shape, F32)
    to_next[...] = jnp.zeros(to_next.shape, F32)
    for at, field in enumerate(fields):
        to_prev[HALO * at : HALO * at + HALO, :] = field[:HALO]
        to_next[HALO * at : HALO * at + HALO, :] = field[lon_rows - HALO :]
        low = pltpu.roll(field[:, :LANES], 6 * at, 1) if at else field[:, :LANES]
        high = pltpu.roll(field[:, width - LANES :], (6 * at + 6) % LANES, 1)
        edges = jnp.where((lane >= 6 * at) & (lane < 6 * at + 3), low, edges)
        edges = jnp.where((lane >= 6 * at + 3) & (lane < 6 * at + 6), high, edges)
    to_prev[27:30, :LANES] = edges[:HALO]
    to_next[27:30, :LANES] = edges[lon_rows - HALO :]
    keep(ocean, fields[8])
    bit = jnp.left_shift(1, iota((8, width), 0))
    sums = {}
    for column in range(2):

        def body(row, carry):
            wet = same_row(ocean, row, 0)
            out = []
            for word in range(2):
                for level in range(2):
                    held = row_of(bits.at[word, level], row)
                    out.append(carry[word * 2 + level] + jnp.where((held & bit) != 0, wet, -wet))
            return tuple(out)

        zero = jnp.zeros((8, width), F32)
        got = lax.fori_loop(column * BLK, column * BLK + BLK, body, (zero,) * 4, unroll=4)
        for word in range(2):
            for level in range(2):
                sums[column, word, level] = got[word * 2 + level]
        for level in range(2):
            held = slice(column * BLK, column * BLK + BLK)
            sums[column, 2, level] = first_row(
                jnp.sum(fields[8][held] * fields[level][held], axis=0, keepdims=True)
            )
    rows = [
        jnp.concatenate([sums[column, group, level] for column in range(2) for group in range(3)], axis=0)
        for level in range(2)
    ]
    found = block_sums(lat_at, rows)
    own[...] = jnp.zeros(own.shape, F32)
    own[TOP : TOP + lon_rows, :] = edges
    own[24:72, :] = own[24:72, :] + found
    for target, at in ((to_prev, 0), (to_next, 24)):
        target[32:40, :LANES] = found[at : at + 8]
        target[32:40, LANES : 2 * LANES] = found[at + 8 : at + 16]
        target[40:48, :LANES] = found[at + 16 : at + 24]


def merge_kernel(own, from_prev, from_next, out):
    out[...] = own[...]
    for source, row, at in ((from_prev, TOP - HALO, 0), (from_next, TOP + 64, 72)):
        out[row : row + HALO, :] = out[row : row + HALO, :] + source[27:30, :LANES]
        out[at : at + 8, :] = out[at : at + 8, :] + source[32:40, :LANES]
        out[at + 8 : at + 16, :] = out[at + 8 : at + 16, :] + source[32:40, LANES : 2 * LANES]
        out[at + 16 : at + 24, :] = out[at + 16 : at + 24, :] + source[40:48, :LANES]


def spread_kernel(coarse, spread):
    lat_at = lax.axis_index("lat")
    wide = spread.shape[2]
    own = wide - LANES
    per = own // BLK
    lane = iota((32, wide), 1)
    block = jnp.where(lane < own, lane // BLK, -1000)
    block = jnp.where((lane >= own) & (lane < own + HALO), per, block)
    block = jnp.where(lane >= wide - HALO, -1, block)
    chosen = jnp.where(iota((32, wide), 0) == block + per * lat_at, 1.0, 0.0).astype(F32)
    for level in range(2):
        spread[level, 0:64, :] = jnp.zeros((64, wide), F32)
        for other in range(2):
            part = lax.dot_general(
                coarse[level, :, other, :],
                chosen,
                (((0,), (0,)), ((), ())),
                precision=EXACT,
                preferred_element_type=F32,
            )
            for group in range(4):
                at = 64 + 16 * group + 8 * other
                spread[level, at : at + 8, :] = part[8 * group : 8 * group + 8]


def corrections(gathered, spread, probe_part, first_part):
    total = gathered[0] + gathered[1] + gathered[2] + gathered[3]
    total = jnp.where(iota(total.shape, 1) >= 64, total, 0.0)
    for level in range(2):
        found = jnp.dot(total, spread[level], precision=EXACT, preferred_element_type=F32)
        probe_part[level] = found
        wide = found.shape[1]
        for low, high, at in ((TOP - HALO, TOP, 16), (TOP, 40, 40), (40, 72, 64), (72, 72 + HALO, 88)):
            for tile in range(wide // LANES):
                line = found[at : at + 1, tile * LANES : tile * LANES + LANES]
                first_part[level, tile, low:high, :] = jnp.broadcast_to(line, (high - low, LANES))


def stencil(centre, above, below, other, coef, ocean):
    wide = centre.shape[1]
    beside = (above + below) + (pltpu.roll(centre, 1, 1) + pltpu.roll(centre, wide - 1, 1))
    return ocean * (coef * centre - beside - 0.5 * other)


SEGMENTS = ((TOP - HALO, TOP, 0), (TOP, 40, 1), (40, 72, 2), (72, 72 + HALO, 3))


def image_kernel(
    obs, kap, bits, land, from_prev, from_next, gathered, spread,
    signed, first_dir, image, first_image, sums_low, sums_high, totals,
    ocean, coef, jacobi, first_rhs,
    word_bits, direction, inner, first_direction, first_inner, probe_part, first_part,
):
    lat_at = lax.axis_index("lat")
    lat_count = lax.axis_size("lat")
    lon_rows, width = land.shape
    wide = width + LANES
    rows = ocean.shape[1]
    lane = iota((rows, LANES), 1)
    before = gathered[jnp.maximum(lat_at - 1, 0), 0:rows, :]
    after = gathered[jnp.minimum(lat_at + 1, lat_count - 1), 0:rows, :]
    take_before = (lane >= LANES - HALO) & (lat_at > 0)
    take_after = (lane < HALO) & (lat_at < lat_count - 1)

    def extended(at, field):
        left = pltpu.roll(before, (LANES - HALO - 6 * at - 3) % LANES, 1)
        right = pltpu.roll(after, -6 * at % LANES, 1) if at else after
        tile = jnp.where(take_before, left, jnp.where(take_after, right, 0.0))
        ends = jnp.zeros((TOP - HALO, width), F32)
        main = jnp.concatenate(
            [
                ends,
                from_prev[HALO * at : HALO * at + HALO, :],
                field,
                from_next[HALO * at : HALO * at + HALO, :],
                ends,
            ],
            axis=0,
        )
        return jnp.concatenate([main, tile], axis=1)

    fields = raw_fields(obs, kap, bits, land)
    wet = extended(8, fields[8])
    keep(ocean, wet)
    for level in range(2):
        value = extended(2 + level, fields[2 + level]) + 5.0
        keep(coef.at[level], value)
        keep(jacobi.at[level], wet / (value * value + 4.0))
        keep(first_rhs.at[level], wet * extended(level, fields[level]))
        for word in range(2):
            at = 4 + word * 2 + level
            keep(word_bits.at[word, level], extended(at, fields[at]).astype(jnp.int32))
    corrections(gathered, spread, probe_part, first_part)
    bit = jnp.left_shift(1, iota((8, wide), 0))
    zero = jnp.zeros((8, width), F32)

    gamma = (zero, zero)
    for low, high, column in SEGMENTS:
        own = column in (1, 2)

        def body(row, carry, column=column, own=own):
            sea = same_row(ocean, row, 0)
            carry = list(carry)
            for level in range(2):
                weight = same_row(jacobi.at[level], row, 0)
                for word in range(2):
                    held = same_row(word_bits.at[word, level], row, 0)
                    rhs = jnp.where((held & bit) != 0, sea, -sea)
                    at = column * 24 + word * 8
                    value = weight * rhs + sea * probe_part[level, at : at + 8, :]
                    direction[level, word, row - (TOP - HALO)] = value
                    if own:
                        both = (rhs * value)[:, :width]
                        signed[level, word, row - TOP] = both
                        carry[word] = carry[word] + both
            return tuple(carry)

        gamma = lax.fori_loop(low, high, body, gamma)
    first_gamma = zero
    for step in range(14):
        row = TOP - HALO + step
        sea = same_row(ocean, row, 8)
        for level in range(2):
            rhs = same_row(first_rhs.at[level], row, 8)
            value = same_row(jacobi.at[level], row, 8) * rhs + sea * same_row(first_part.at[level], row, 8)
            first_direction[level, step] = value
            if HALO <= step < HALO + 8:
                first_dir[level, step - HALO] = value[:, :width]
                first_gamma = first_gamma + (rhs * value)[:, :width]

    def apply_first(row, carry, own):
        sea = same_row(ocean, row, 0)
        carry = list(carry)
        for level in range(2):
            scale = same_row(coef.at[level], row, 0)
            for word in range(2):
                at = row - (TOP - HALO)
                value = stencil(
                    direction[level, word, at],
                    direction[level, word, at - 1],
                    direction[level, word, at + 1],
                    direction[1 - level, word, at],
                    scale,
                    sea,
                )
                inner[level, word, at] = value
                if own:
                    part = value[:, :width]
                    carry[word] = carry[word] + part * part
        return tuple(carry)

    norm = (zero, zero)
    norm = lax.fori_loop(TOP - 2, TOP, functools.partial(apply_first, own=False), norm)
    norm = lax.fori_loop(TOP, TOP + lon_rows, functools.partial(apply_first, own=True), norm)
    norm = lax.fori_loop(
        TOP + lon_rows, TOP + lon_rows + 2, functools.partial(apply_first, own=False), norm
    )
    first_norm = zero
    for step in range(1, 13):
        row = TOP - HALO + step
        sea = same_row(ocean, row, 8)
        for level in range(2):
            value = stencil(
                first_direction[level, step],
                first_direction[level, step - 1],
                first_direction[level, step + 1],
                first_direction[1 - level, step],
                same_row(coef.at[level], row, 8),
                sea,
            )
            first_inner[level, step] = value
            if HALO <= step < HALO + 8:
                part = value[:, :width]
                first_norm = first_norm + part * part

    def apply_second(row, carry, own):
        sea = same_row(ocean, row, 0)
        carry = list(carry)
        for level in range(2):
            scale = same_row(coef.at[level], row, 0)
            for word in range(2):
                at = row - (TOP - HALO)
                value = stencil(
                    inner[level, word, at],
                    inner[level, word, at - 1],
                    inner[level, word, at + 1],
                    inner[1 - level, word, at],
                    scale,
                    sea,
                )
                image[level, word, row - (TOP - 1)] = value
                if own:
                    carry[level * 2 + word] = carry[level * 2 + word] + value[:, :width]
        return tuple(carry)

    none = (zero,) * 4
    lax.fori_loop(TOP - 1, TOP, functools.partial(apply_second, own=False), none)
    sums = {}
    for column in range(2):
        low = TOP + column * BLK
        got = lax.fori_loop(low, low + BLK, functools.partial(apply_second, own=True), none)
        for level in range(2):
            for word in range(2):
                sums[column, word, level] = got[level * 2 + word]
    lax.fori_loop(TOP + lon_rows, TOP + lon_rows + 1, functools.partial(apply_second, own=False), none)
    first_sum = [zero, zero]
    for step in range(2, 12):
        row = TOP - HALO + step
        sea = same_row(ocean, row, 8)
        for level in range(2):
            value = stencil(
                first_inner[level, step],
                first_inner[level, step - 1],
                first_inner[level, step + 1],
                first_inner[1 - level, step],
                same_row(coef.at[level], row, 8),
                sea,
            )
            first_image[level, step - 2] = value
            if HALO <= step < HALO + 8:
                first_sum[level] = first_sum[level] + value[:, :width]
    for level in range(2):
        for column in range(2):
            half = first_sum[level][column * 4 : column * 4 + 4]
            sums[column, 2, level] = first_row(jnp.sum(half, axis=0, keepdims=True))
    stacked = [
        jnp.concatenate([sums[column, group, level] for column in range(2) for group in range(3)], axis=0)
        for level in range(2)
    ]
    found = block_sums(lat_at, stacked)
    sums_low[...] = found[:24]
    sums_high[...] = found[24:]
    for at, value in enumerate((gamma[0], gamma[1], first_gamma, norm[0], norm[1], first_norm)):
        totals[at] = value[:, :LANES] + value[:, LANES:]


def second_kernel(
    gathered, spread, image, first_image, totals, ocean, coef, jacobi,
    packed, second, first_second,
    held, first_held, probe_part, first_part,
):
    width = second.shape[-1]
    lon_rows = second.shape[2]
    corrections(gathered, spread, probe_part, first_part)
    zero = jnp.zeros((8, width), F32)
    cross = (zero, zero)
    for low, high, column in ((TOP - 1, TOP, 0), (TOP, 40, 1), (40, 72, 2), (72, 73, 3)):
        own = column in (1, 2)

        def body(row, carry, column=column, own=own):
            sea = same_row(ocean, row, 0)
            carry = list(carry)
            for level in range(2):
                weight = same_row(jacobi.at[level], row, 0)
                for word in range(2):
                    at = column * 24 + word * 8
                    source = image[level, word, row - (TOP - 1)]
                    value = weight * source + sea * probe_part[level, at : at + 8, :]
                    held[level, word, row - (TOP - 1)] = value
                    if own:
                        second[level, word, row - TOP] = value[:, :width]
                        carry[word] = carry[word] + (value * source)[:, :width]
            return tuple(carry)

        cross = lax.fori_loop(low, high, body, cross)
    first_cross = zero
    for step in range(10):
        row = TOP - 1 + step
        sea = same_row(ocean, row, 8)
        for level in range(2):
            source = first_image[level, step]
            value = same_row(jacobi.at[level], row, 8) * source + sea * same_row(
                first_part.at[level], row, 8
            )
            first_held[level, step] = value
            if 1 <= step < 9:
                first_second[level, step - 1] = value[:, :width]
                first_cross = first_cross + (value * source)[:, :width]

    def apply(row, carry):
        sea = same_row(ocean, row, 0)
        carry = list(carry)
        for level in range(2):
            scale = same_row(coef.at[level], row, 0)
            for word in range(2):
                at = row - (TOP - 1)
                value = stencil(
                    held[level, word, at],
                    held[level, word, at - 1],
                    held[level, word, at + 1],
                    held[1 - level, word, at],
                    scale,
                    sea,
                )[:, :width]
                carry[word] = carry[word] + value * value
        return tuple(carry)

    norm = lax.fori_loop(TOP, TOP + lon_rows, apply, (zero, zero))
    first_norm = zero
    for step in range(1, 9):
        row = TOP - 1 + step
        sea = same_row(ocean, row, 8)
        for level in range(2):
            value = stencil(
                first_held[level, step],
                first_held[level, step - 1],
                first_held[level, step + 1],
                first_held[1 - level, step],
                same_row(coef.at[level], row, 8),
                sea,
            )[:, :width]
            first_norm = first_norm + value * value
    found = [totals[at] for at in range(6)] + [
        value[:, :LANES] + value[:, LANES:]
        for value in (cross[0], cross[1], first_cross, norm[0], norm[1], first_norm)
    ]
    lane = iota((8, LANES), 1)
    probe = iota((8, LANES), 0)
    out = jnp.zeros((8, LANES), F32)
    for kind in range(4):
        for group in range(3):
            total = jnp.broadcast_to(
                jnp.sum(found[kind * 3 + group], axis=1, keepdims=True), (8, LANES)
            )
            place = lane == (64 + kind if group == 2 else (kind * 2 + group) * 8 + probe)
            out = out + jnp.where(place, total, 0.0)
    packed[...] = jnp.broadcast_to(jnp.sum(out, axis=0, keepdims=True), packed.shape)


def sign_kernel(second, bits, land, out, ocean):
    lon_rows, width = land.shape
    keep(ocean, land[...].astype(F32))
    bit = jnp.left_shift(1, iota((8, width), 0))

    def body(row, carry):
        sea = same_row(ocean, row, 0)
        for level in range(2):
            for word in range(2):
                held = row_of(bits.at[word, level], row)
                out[level, word, row] = jnp.where((held & bit) != 0, sea, -sea) * second[level, word, row]
        return carry

    lax.fori_loop(0, lon_rows, body, 0, unroll=2)


def finish_kernel(packed, signed, signed_second, first_dir, first_second, kap, solution, diagonal, residual, natural):
    width = kap.shape[-1]
    lon_rows = kap.shape[1]
    total = jnp.broadcast_to(jnp.sum(packed[...], axis=0, keepdims=True), (8, LANES))
    lane = iota((8, LANES), 1)
    probe = iota((8, LANES), 0)

    def weights(group):
        found = []
        for kind in range(4):
            place = lane == (64 + kind if group == 2 else (kind * 2 + group) * 8 + probe)
            found.append(
                jnp.broadcast_to(
                    jnp.sum(jnp.where(place, total, 0.0), axis=1, keepdims=True), (8, LANES)
                )
            )
        gamma, norm, cross, second = found
        ratio = cross / norm
        rest = second - ratio * cross
        alive = rest > 0.0
        later = jnp.where(alive, (norm - ratio * gamma) / jnp.where(alive, rest, 1.0), 0.0)
        earlier = gamma / norm - later * ratio
        return (
            jnp.concatenate([earlier] * (width // LANES), axis=1),
            jnp.concatenate([later] * (width // LANES), axis=1),
        )

    low, high, first = weights(0), weights(1), weights(2)

    def body(row, carry):
        for level in range(2):
            value = (
                low[0] * signed[level, 0, row]
                + low[1] * signed_second[level, 0, row]
                + high[0] * signed[level, 1, row]
                + high[1] * signed_second[level, 1, row]
            )
            diagonal[level, pl.ds(row, 1), :] = jnp.sum(value, axis=0, keepdims=True) / PROBES
        return carry

    lax.fori_loop(0, lon_rows, body, 0, unroll=4)
    for level in range(2):
        for step in range(8):
            value = first[0] * first_dir[level, step] + first[1] * first_second[level, step]
            for tile in range(width // LANES):
                natural[level, tile, pl.ds(step, 8, stride=8), :] = value[:, tile * LANES : tile * LANES + LANES]
        solution[level] = jnp.concatenate([natural[level, tile] for tile in range(width // LANES)], axis=1)
        coef = kap[level] + 5.0
        bound = 0.5 / (coef * coef + 4.0)
        residual[level] = solution[level] / jnp.maximum(diagonal[level], bound)


def call(kernel, outs, scratch=(), limit=24, cost=None):
    return functools.partial(
        _run, kernel, outs, scratch, limit, cost
    )


def _run(kernel, outs, scratch, limit, cost, *args):
    return pl.pallas_call(
        kernel,
        out_shape=outs,
        in_specs=vmem(len(args)),
        out_specs=tuple(vmem(len(outs))),
        scratch_shapes=list(scratch),
        compiler_params=pltpu.CompilerParams(vmem_limit_bytes=limit << 20),
        cost_estimate=cost,
    )(*args)


def per_device(observed, kappa_squared, probe_bits, land_sea, coarse_block_inverse):
    lon_rows, width = land_sea.shape
    wide = width + LANES
    rows = lon_rows + 2 * TOP
    lon_count = lax.axis_size("lon")
    lat_count = lax.axis_size("lat")
    onward = [(i, (i + 1) % lon_count) for i in range(lon_count)]
    back = [((i + 1) % lon_count, i) for i in range(lon_count)]
    raw = (observed, kappa_squared, probe_bits, land_sea)

    to_prev, to_next, own = call(
        prepare_kernel,
        (shape(48, width), shape(48, width), shape(96, LANES)),
        [pltpu.VMEM((width // LANES, lon_rows, LANES), F32)],
    )(*raw)
    from_prev = lax.ppermute(to_next, "lon", onward)
    from_next = lax.ppermute(to_prev, "lon", back)
    (spread,) = call(spread_kernel, (shape(2, LANES, wide),))(coarse_block_inverse)
    (merged,) = call(merge_kernel, (shape(96, LANES),))(own, from_prev, from_next)
    gathered = lax.all_gather(merged, "lat")
    probe_parts = pltpu.VMEM((2, 96, wide), F32)
    tiles = wide // LANES
    first_parts = pltpu.VMEM((2, tiles, rows, LANES), F32)
    (
        signed, first_dir, image, first_image, sums_low, sums_high, totals,
        ocean, coef, jacobi, _,
    ) = call(
        image_kernel,
        (
            shape(2, 2, lon_rows, 8, width),
            shape(2, 8, 8, width),
            shape(2, 2, lon_rows + 2, 8, wide),
            shape(2, 10, 8, wide),
            shape(24, LANES),
            shape(24, LANES),
            shape(6, 8, LANES),
            shape(tiles, rows, LANES),
            shape(2, tiles, rows, LANES),
            shape(2, tiles, rows, LANES),
            shape(2, tiles, rows, LANES),
        ),
        [
            pltpu.VMEM((2, 2, tiles, rows, LANES), jnp.int32),
            pltpu.VMEM((2, 2, lon_rows + 2 * HALO, 8, wide), F32),
            pltpu.VMEM((2, 2, lon_rows + 2 * HALO, 8, wide), F32),
            pltpu.VMEM((2, 14, 8, wide), F32),
            pltpu.VMEM((2, 14, 8, wide), F32),
            probe_parts,
            first_parts,
        ],
    )(*raw, from_prev, from_next, gathered, spread)

    sums_prev = lax.ppermute(sums_high, "lon", onward)
    sums_next = lax.ppermute(sums_low, "lon", back)
    sums = lax.all_gather(jnp.concatenate([sums_prev, sums_low, sums_high, sums_next], axis=0), "lat")
    packed, second, first_second = call(
        second_kernel,
        (
            shape(lon_count * lat_count, LANES),
            shape(2, 2, lon_rows, 8, width),
            shape(2, 8, 8, width),
        ),
        [
            pltpu.VMEM((2, 2, lon_rows + 2, 8, wide), F32),
            pltpu.VMEM((2, 10, 8, wide), F32),
            probe_parts,
            first_parts,
        ],
    )(sums, spread, image, first_image, totals, ocean, coef, jacobi)
    everyone = lax.all_to_all(packed, ("lon", "lat"), 0, 0)
    (signed_second,) = call(
        sign_kernel,
        (shape(2, 2, lon_rows, 8, width),),
        [pltpu.VMEM((width // LANES, lon_rows, LANES), F32)],
    )(second, probe_bits, land_sea)
    return tuple(
        call(
            finish_kernel,
            (shape(2, lon_rows, width),) * 3,
            [pltpu.VMEM((2, width // LANES, lon_rows, LANES), F32)],
        )(
            everyone, signed, signed_second, first_dir, first_second, kappa_squared
        )
    )


def solution(mesh):
    placed = (
        P(None, "lon", "lat"),
        P(None, "lon", "lat"),
        P(None, None, "lon", "lat"),
        P("lon", "lat"),
        P(),
    )
    return jax.shard_map(
        per_device,
        mesh=mesh,
        in_specs=placed,
        out_specs=(P(None, "lon", "lat"), P(None, "lon", "lat"), P(None, "lon", "lat")),
        check_vma=False,
    )
```

profile of v0, /device:TPU:1, one launch (start us, length us, event | category | flops | bytes accessed | tf_op | source)
XLA Modules:
  0.0 94.8 jit_solution(11736041768403311422)
XLA Ops:
  0.6 0.0 copy-start
  0.6 0.9 copy-done
  1.6 0.0 copy-start.6
  1.6 0.9 copy-done.6
  2.5 0.0 copy-start.9
  2.5 0.8 copy-done.9
  3.3 0.0 copy-start.11
  3.3 0.9 copy-done.11
  4.2 0.9 shard_map.76
  5.1 2.1 %collective-permute-start = (f32[48,256]{1,0:T(8,128)S(1)}, f32[48,256]{1,0:T(8,128)S(1)}, u32[]{:S(2)}, u32[]{:S(2)}) collective-permute-start(f32[48,256]{1,0:T(8,128)S(1)} %get-tuple-element.19), channel_id=1, source_target_pairs={{0,4},{4,8},{8,12},{12,16},{16,20},{20,24},{24,28},{28,32},{32,36}... | collective-permute-start | bytes 147464 | tf_op jit(solution)/shard_map/ppermute | solution.py:576
  7.2 7.7 %collective-permute-start.1 = (f32[48,256]{1,0:T(8,128)S(1)}, f32[48,256]{1,0:T(8,128)S(1)}, u32[]{:S(2)}, u32[]{:S(2)}) collective-permute-start(f32[48,256]{1,0:T(8,128)S(1)} %get-tuple-element.20), channel_id=1, source_target_pairs={{4,0},{8,4},{12,8},{16,12},{20,16},{24,20},{28,24},{32,28},{36,32}... | collective-permute-start | bytes 147464 | tf_op jit(solution)/shard_map/ppermute | solution.py:577
  14.9 0.0 copy-start.13
  14.9 0.8 copy-done.13
  15.7 0.4 shard_map.78.spread
  16.2 0.1 collective-permute-done.from_prev
  16.3 0.0 collective-permute-done.1.from_next
  16.3 8.5 %all-gather = f32[384,128]{1,0:T(8,128)S(1)} all-gather(f32[96,128]{1,0:T(8,128)S(1)} %shard_map.77), channel_id=2, replica_groups=mesh['lon'=64,'lat'=4] {'lat'}, dimensions={0}, use_global_device_ids=true | all-gather | bytes 245760 | tf_op jit(solution)/shard_map/all_gather | solution.py:580
  24.8 0.0 copy-start.7
  24.8 0.9 copy-done.7
  25.7 0.0 copy-start.12
  25.7 0.9 copy-done.12
  26.6 16.6 %shard_map.79 = (f32[2,2,64,8,256]{4,3,2,1,0:T(8,128)S(1)}, f32[2,8,8,256]{3,2,1,0:T(8,128)S(1)}, f32[2,2,66,8,384]{4,3,2,1,0:T(8,128)S(1)}, f32[2,10,8,384]{3,2...) custom-call(f32[2,64,256]{2,1,0:T(8,128)S(1)} %copy-done.12, ...), custom_call_target="tpu_custom_call" | custom-call | tf_op jit(solution)/shard_map/pallas_call | solution.py:550
  43.2 0.0 copy-start.2
  43.2 0.0 collective-permute-start.2
  43.3 6.0 %collective-permute-start.3 = (f32[24,128]{1,0:T(8,128)S(1)}, f32[24,128]{1,0:T(8,128)S(1)}, u32[]{:S(2)}, u32[]{:S(2)}) collective-permute-start(f32[24,128]{1,0:T(8,128)S(1)} %get-tuple-element.23), channel_id=1, source_target_pairs={{4,0},{8,4},{12,8},{16,12},{20,16},{24,20},{28,24},{32,28},{36,32}... | collective-permute-start | bytes 36872 | tf_op jit(solution)/shard_map/ppermute | solution.py:614
  49.3 1.1 %collective-permute-done.2 = f32[24,128]{1,0:T(8,128)S(1)} collective-permute-done((f32[24,128]{1,0:T(8,128)S(1)}, f32[24,128]{1,0:T(8,128)S(1)}, u32[]{:S(2)}, u32[]{:S(2)}) %collective-permute-start.2) | collective-permute-done | bytes 12320 | tf_op jit(solution)/shard_map/ppermute | solution.py:613
  50.4 0.0 collective-permute-done.3
  50.4 8.0 %all-gather.1 = f32[384,128]{1,0:T(8,128)S(1)} all-gather(f32[96,128]{1,0:T(8,128)S(1)} %pad_maximum_fusion), channel_id=3, replica_groups=mesh['lon'=64,'lat'=4] {'lat'}, dimensions={0}, use_global_device_ids=true | all-gather | bytes 245760 | tf_op jit(solution)/shard_map/all_gather | solution.py:615
  58.4 0.0 copy-start.1
  58.4 0.0 copy-start.10
  58.4 9.1 %shard_map.80 = (f32[256,128]{1,0:T(8,128)}, f32[2,2,64,8,256]{4,3,2,1,0:T(8,128)S(1)}, f32[2,8,8,256]{3,2,1,0:T(8,128)S(1)}) custom-call(f32[4,96,128]{2,1,0:T(8,128)S(1)} %bitcast.6, f32[2,128,384]{2,1,0:T(8,128)S(1)} %shard_map.78.spread, f32[2,2,66,8,384]{4,3,2,1,0:T(8,128)S(1)} %get-tuple-element.24.image, ...), custom_call_target="tpu_custom_call" | custom-call | tf_op jit(solution)/shard_map/pallas_call | solution.py:550
  67.5 0.0 copy-done.2
  67.5 0.0 copy-start.4
  67.5 1.3 %copy-done.4 = f32[2,2,64,8,256]{4,3,2,1,0:T(8,128)} copy-done((f32[2,2,64,8,256]{4,3,2,1,0:T(8,128)}, f32[2,2,64,8,256]{4,3,2,1,0:T(8,128)S(1)}, u32[]{:S(2)}) %copy-start.4) | copy-done | bytes 2097176
  68.8 9.9 %all-to-all-start = ((f32[256,1,128]{2,1,0:T(1,128)}), f32[256,1,128]{2,1,0:T(1,128)S(1)}, u32[]{:S(2)}, u32[]{:S(2)}) async-start(f32[256,1,128]{2,1,0:T(1,128)} %bitcast.3), calls=%async_computation | async-start | bytes 262144 | tf_op jit(solution)/shard_map/all_to_all | solution.py:630
  78.7 0.0 copy-done.1
  78.7 0.0 copy-done.10
  78.7 0.0 copy-start.5
  78.7 1.6 %copy-done.5 = f32[2,2,64,8,256]{4,3,2,1,0:T(8,128)S(1)} copy-done((f32[2,2,64,8,256]{4,3,2,1,0:T(8,128)S(1)}, f32[2,2,64,8,256]{4,3,2,1,0:T(8,128)}, u32[]{:S(2)}) %copy-start.5) | copy-done | bytes 2097176
  80.3 0.0 copy-start.8
  80.3 0.5 shard_map.81.signed_second
  80.8 10.9 %all-to-all-done = f32[256,1,128]{2,1,0:T(1,128)S(1)} async-done(((f32[256,1,128]{2,1,0:T(1,128)}), f32[256,1,128]{2,1,0:T(1,128)S(1)}, u32[]{:S(2)}, u32[]{:S(2)}) %all-to-all-start) | async-done | bytes 131104 | tf_op jit(solution)/shard_map/all_to_all | solution.py:630
  91.7 0.0 copy-done.8
  91.7 0.0 copy-start.3
  91.7 1.6 %copy-done.3 = f32[2,2,64,8,256]{4,3,2,1,0:T(8,128)S(1)} copy-done((f32[2,2,64,8,256]{4,3,2,1,0:T(8,128)S(1)}, f32[2,2,64,8,256]{4,3,2,1,0:T(8,128)}, u32[]{:S(2)}) %copy-start.3) | copy-done | bytes 2097176
  93.3 1.6 %shard_map.82 = (f32[2,64,256]{2,1,0:T(8,128)}, f32[2,64,256]{2,1,0:T(8,128)}, f32[2,64,256]{2,1,0:T(8,128)}) custom-call(f32[256,128]{1,0:T(8,128)S(1)} %bitcast.8, f32[2,2,64,8,256]{4,3,2,1,0:T(8,128)S(1)} %copy-done.3, f32[2,2,64,8,256]{4,3,2,1,0:T(8,128)S(1)} %shard_map.81.signed_second, f32[2,8,8,256]{3,2,1,0:T(8,128)S(1)} %get-tuple-element.33.first_dir, ...), custom_call_target="tpu_custom_call" | custom-call | tf_op jit(solution)/shard_map/pallas_call | solution.py:550
  (2 shorter events, 0.0 us)
Async XLA Ops:
  0.6 1.0 %copy-start = (s32[2,2,64,256]{3,2,1,0:T(8,128)S(1)}, s32[2,2,64,256]{3,2,1,0:T(8,128)}, u32[]{:S(2)}) copy-start(s32[2,2,64,256]{3,2,1,0:T(8,128)} %bits.5) | copy-start | bytes 786436
  1.6 0.9 copy-start.6
  2.5 0.8 copy-start.9
  3.3 0.9 copy-start.11
  5.1 11.2 %collective-permute-start = (f32[48,256]{1,0:T(8,128)S(1)}, f32[48,256]{1,0:T(8,128)S(1)}, u32[]{:S(2)}, u32[]{:S(2)}) collective-permute-start(f32[48,256]{1,0:T(8,128)S(1)} %get-tuple-element.19), channel_id=1, source_target_pairs={{0,4},{4,8},{8,12},{12,16},{16,20},{20,24},{24,28},{28,32},{32,36}... | collective-permute-start | bytes 147464 | tf_op jit(solution)/shard_map/ppermute | solution.py:576
  7.2 9.1 %collective-permute-start.1 = (f32[48,256]{1,0:T(8,128)S(1)}, f32[48,256]{1,0:T(8,128)S(1)}, u32[]{:S(2)}, u32[]{:S(2)}) collective-permute-start(f32[48,256]{1,0:T(8,128)S(1)} %get-tuple-element.20), channel_id=1, source_target_pairs={{4,0},{8,4},{12,8},{16,12},{20,16},{24,20},{28,24},{32,28},{36,32}... | collective-permute-start | bytes 147464 | tf_op jit(solution)/shard_map/ppermute | solution.py:577
  14.9 0.8 copy-start.13
  24.8 0.9 copy-start.7
  25.7 0.9 copy-start.12
  43.2 24.2 %copy-start.2 = (f32[2,2,64,8,256]{4,3,2,1,0:T(8,128)}, f32[2,2,64,8,256]{4,3,2,1,0:T(8,128)S(1)}, u32[]{:S(2)}) copy-start(f32[2,2,64,8,256]{4,3,2,1,0:T(8,128)S(1)} %get-tuple-element.31.signed) | copy-start | bytes 6291460
  43.2 7.1 %collective-permute-start.2 = (f32[24,128]{1,0:T(8,128)S(1)}, f32[24,128]{1,0:T(8,128)S(1)}, u32[]{:S(2)}, u32[]{:S(2)}) collective-permute-start(f32[24,128]{1,0:T(8,128)S(1)} %get-tuple-element.22), channel_id=1, source_target_pairs={{0,4},{4,8},{8,12},{12,16},{16,20},{20,24},{24,28},{28,32},{32,36}... | collective-permute-start | bytes 36872 | tf_op jit(solution)/shard_map/ppermute | solution.py:613
  43.3 7.1 %collective-permute-start.3 = (f32[24,128]{1,0:T(8,128)S(1)}, f32[24,128]{1,0:T(8,128)S(1)}, u32[]{:S(2)}, u32[]{:S(2)}) collective-permute-start(f32[24,128]{1,0:T(8,128)S(1)} %get-tuple-element.23), channel_id=1, source_target_pairs={{4,0},{8,4},{12,8},{16,12},{20,16},{24,20},{28,24},{32,28},{36,32}... | collective-permute-start | bytes 36872 | tf_op jit(solution)/shard_map/ppermute | solution.py:614
  58.4 20.3 %copy-start.1 = (s32[2,2,64,256]{3,2,1,0:T(8,128)S(1)}, s32[2,2,64,256]{3,2,1,0:T(8,128)}, u32[]{:S(2)}) copy-start(s32[2,2,64,256]{3,2,1,0:T(8,128)} %bits.5) | copy-start | bytes 786436
  58.4 20.3 %copy-start.10 = (s32[64,256]{1,0:T(8,128)S(1)}, s32[64,256]{1,0:T(8,128)}, u32[]{:S(2)}) copy-start(s32[64,256]{1,0:T(8,128)} %land.5) | copy-start | bytes 196612
  67.5 1.3 %copy-start.4 = (f32[2,2,64,8,256]{4,3,2,1,0:T(8,128)}, f32[2,2,64,8,256]{4,3,2,1,0:T(8,128)S(1)}, u32[]{:S(2)}) copy-start(f32[2,2,64,8,256]{4,3,2,1,0:T(8,128)S(1)} %get-tuple-element.32.second) | copy-start | bytes 6291460
  68.8 22.9 %all-to-all-start = ((f32[256,1,128]{2,1,0:T(1,128)}), f32[256,1,128]{2,1,0:T(1,128)S(1)}, u32[]{:S(2)}, u32[]{:S(2)}) async-start(f32[256,1,128]{2,1,0:T(1,128)} %bitcast.3), calls=%async_computation | async-start | bytes 262144 | tf_op jit(solution)/shard_map/all_to_all | solution.py:630
  78.7 1.6 %copy-start.5 = (f32[2,2,64,8,256]{4,3,2,1,0:T(8,128)S(1)}, f32[2,2,64,8,256]{4,3,2,1,0:T(8,128)}, u32[]{:S(2)}) copy-start(f32[2,2,64,8,256]{4,3,2,1,0:T(8,128)} %copy-done.4) | copy-start | bytes 6291460
  80.3 11.4 %copy-start.8 = (f32[2,64,256]{2,1,0:T(8,128)S(1)}, f32[2,64,256]{2,1,0:T(8,128)}, u32[]{:S(2)}) copy-start(f32[2,64,256]{2,1,0:T(8,128)} %kap.5) | copy-start | bytes 393220
  91.7 1.6 %copy-start.3 = (f32[2,2,64,8,256]{4,3,2,1,0:T(8,128)S(1)}, f32[2,2,64,8,256]{4,3,2,1,0:T(8,128)}, u32[]{:S(2)}) copy-start(f32[2,2,64,8,256]{4,3,2,1,0:T(8,128)} %copy-done.2) | copy-start | bytes 6291460
where the time goes:
time: 95.2 us; the launch traced here: 94.8 us
  Pallas kernels  29.1 us (31%)
  starting transfers between devices  25.7 us (27%)
  blocking collectives  16.5 us (17%)
  waiting for transfers between devices  12.1 us (13%)
  local copies, waits for them, and re-layouts  10.7 us (11%)
    pallas_call x7, Pallas kernels, _run(): pl.pallas_call(kernel, out_shape=outs, in_specs=vmem(len(args)), out_spec...  29.1 us
    all_to_all x1, waiting for transfers between devices, per_device(): everyone = lax.all_to_all(packed, ('lon', 'lat'), 0, 0)  10.9 us
    unnamed x28, local copies, waits for them, and re-layouts  10.7 us
    all_to_all x1, starting transfers between devices, per_device(): everyone = lax.all_to_all(packed, ('lon', 'lat'), 0, 0)  9.88 us
    all_gather x1, blocking collectives, per_device(): gathered = lax.all_gather(merged, 'lat')  8.49 us
    all_gather x1, blocking collectives, per_device(): lax.all_gather(jnp.concatenate([sums_prev, sums_low, sums_high, sums_next...  7.98 us
    ppermute x1, starting transfers between devices, per_device(): from_next = lax.ppermute(to_prev, 'lon', back)  7.66 us
    ppermute x1, starting transfers between devices, per_device(): sums_next = lax.ppermute(sums_low, 'lon', back)  6.04 us
  transfers between devices with their start and end apart: 5, of which 3 were waited for; matrix products, arithmetic and copies ran while one was open for 0% of the time, Pallas kernels for 1%

commit v1 on v0

v1 whole, which is shorter than its diff:
```python
import functools

import jax
import jax.numpy as jnp
from jax import lax
from jax.experimental import pallas as pl
from jax.experimental.pallas import tpu as pltpu
from jax.sharding import PartitionSpec as P

BLK = 32
PROBES = 16
HALO = 3
TOP = 8
LANES = 128
EXACT = lax.Precision.HIGHEST
F32 = jnp.float32


def vmem(count):
    return [pl.BlockSpec(memory_space=pltpu.VMEM)] * count


def shape(*dims):
    return jax.ShapeDtypeStruct(dims, F32)


def iota(dims, axis):
    return lax.broadcasted_iota(jnp.int32, dims, axis)


def same_row(ref, row, stride):
    found = []
    for tile in range(ref.shape[0]):
        if stride == 0:
            found.append(ref[tile, pl.ds(row, 8, stride=0), :])
        else:
            found.append(ref[tile, pl.ds(row, 8, stride=stride), :])
    return jnp.concatenate(found, axis=1)


def keep(ref, value):
    for tile in range(ref.shape[0]):
        ref[tile] = value[:, tile * LANES : tile * LANES + LANES]


def row_of(ref, row):
    return jnp.broadcast_to(ref[pl.ds(row, 1), :], (8, ref.shape[1]))


def fetch(sources, targets, sems):
    copies = [
        pltpu.make_async_copy(source, target, sems.at[at])
        for at, (source, target) in enumerate(zip(sources, targets))
    ]
    for copy in copies:
        copy.start()
    for copy in copies:
        copy.wait()


def block_lanes(lat_at, level, width):
    source = iota((width, LANES), 0)
    lane = iota((width, LANES), 1)
    return jnp.where(lane == 64 + 16 * lat_at + 8 * level + source // BLK, 1.0, 0.0).astype(F32)


def block_sums(lat_at, rows):
    total = None
    for level in range(2):
        part = jnp.dot(
            rows[level],
            block_lanes(lat_at, level, rows[level].shape[1]),
            precision=EXACT,
            preferred_element_type=F32,
        )
        total = part if total is None else total + part
    return total


def first_row(row):
    return jnp.where(iota((8, row.shape[1]), 0) == 0, jnp.broadcast_to(row, (8, row.shape[1])), 0.0)


def raw_fields(obs, kap, bits, land):
    return (
        [obs[level] for level in range(2)]
        + [kap[level] for level in range(2)]
        + [bits[word, level].astype(F32) for word in range(2) for level in range(2)]
        + [land[...].astype(F32)]
    )


def prepare_kernel(
    obs_in, kap_in, bits_in, land_in, to_odd, to_even, own,
    obs, kap, bits, land, ocean, sems,
):
    fetch((obs_in, kap_in, bits_in, land_in), (obs, kap, bits, land), sems)
    lat_at = lax.axis_index("lat")
    even = lax.rem(lax.axis_index("lon"), 2) == 0
    lon_rows, width = land.shape
    fields = raw_fields(obs, kap, bits, land)
    lane = iota((lon_rows, LANES), 1)
    edges = jnp.zeros((lon_rows, LANES), F32)
    for at, field in enumerate(fields):
        first, last = field[:HALO], field[lon_rows - HALO :]
        here = slice(HALO * at, HALO * at + HALO)
        to_odd[here, :] = jnp.where(even, first, last)
        to_even[here, :] = jnp.where(even, last, first)
        low = pltpu.roll(field[:, :LANES], 6 * at, 1) if at else field[:, :LANES]
        high = pltpu.roll(field[:, width - LANES :], (6 * at + 6) % LANES, 1)
        edges = jnp.where((lane >= 6 * at) & (lane < 6 * at + 3), low, edges)
        edges = jnp.where((lane >= 6 * at + 3) & (lane < 6 * at + 6), high, edges)
    to_odd[27:30, :LANES] = jnp.where(even, edges[:HALO], edges[lon_rows - HALO :])
    to_even[27:30, :LANES] = jnp.where(even, edges[lon_rows - HALO :], edges[:HALO])
    keep(ocean, fields[8])
    bit = jnp.left_shift(1, iota((8, width), 0))
    zero = jnp.zeros((8, width), F32)
    sums = {}
    for column in range(2):
        for word in range(2):
            for level in range(2):
                sums[column, word, level] = zero

        def body(row, carry):
            wet = same_row(ocean, row, 0)
            out = []
            for word in range(2):
                for level in range(2):
                    held = row_of(bits.at[word, level], row)
                    out.append(carry[word * 2 + level] + jnp.where((held & bit) != 0, wet, -wet))
            return tuple(out)

        got = lax.fori_loop(column * BLK, column * BLK + BLK, body, (zero,) * 4, unroll=BLK)
        for word in range(2):
            for level in range(2):
                sums[column, word, level] = got[word * 2 + level]
        for level in range(2):
            held = slice(column * BLK, column * BLK + BLK)
            sums[column, 2, level] = first_row(
                jnp.sum(fields[8][held] * fields[level][held], axis=0, keepdims=True)
            )
    rows = [
        jnp.concatenate([sums[column, group, level] for column in range(2) for group in range(3)], axis=0)
        for level in range(2)
    ]
    found = block_sums(lat_at, rows)
    own[...] = jnp.zeros(own.shape, F32)
    own[TOP : TOP + lon_rows, :] = edges
    own[24:72, :] = own[24:72, :] + found
    first, last = found[:24], found[24:]
    for target, part in (
        (to_odd, jnp.where(even, first, last)),
        (to_even, jnp.where(even, last, first)),
    ):
        target[32:40, :LANES] = part[:8]
        target[32:40, LANES : 2 * LANES] = part[8:16]
        target[40:48, :LANES] = part[16:24]


def merge_kernel(own, from_odd, from_even, out):
    even = lax.rem(lax.axis_index("lon"), 2) == 0
    odd_part, even_part = from_odd[...], from_even[...]
    prev = jnp.where(even, odd_part, even_part)
    later = jnp.where(even, even_part, odd_part)
    out[...] = own[...]
    for source, row, at in ((prev, TOP - HALO, 0), (later, TOP + 64, 72)):
        out[row : row + HALO, :] = out[row : row + HALO, :] + source[27:30, :LANES]
        out[at : at + 8, :] = out[at : at + 8, :] + source[32:40, :LANES]
        out[at + 8 : at + 16, :] = out[at + 8 : at + 16, :] + source[32:40, LANES : 2 * LANES]
        out[at + 16 : at + 24, :] = out[at + 16 : at + 24, :] + source[40:48, :LANES]


def base_kernel(
    obs_in, kap_in, bits_in, land_in, coarse_in, spread, ocean, coef, jacobi, first_rhs, word_bits,
    obs, kap, bits, land, coarse, sems,
):
    fetch(
        (obs_in, kap_in, bits_in, land_in, coarse_in), (obs, kap, bits, land, coarse), sems
    )
    lat_at = lax.axis_index("lat")
    wide = spread.shape[2]
    width = wide - LANES
    per = width // BLK
    lane = iota((32, wide), 1)
    block = jnp.where(lane < width, lane // BLK, -1000)
    block = jnp.where((lane >= width) & (lane < width + HALO), per, block)
    block = jnp.where(lane >= wide - HALO, -1, block)
    chosen = jnp.where(iota((32, wide), 0) == block + per * lat_at, 1.0, 0.0).astype(F32)
    for level in range(2):
        spread[level, 0:64, :] = jnp.zeros((64, wide), F32)
        for other in range(2):
            part = lax.dot_general(
                coarse[level, :, other, :],
                chosen,
                (((0,), (0,)), ((), ())),
                precision=EXACT,
                preferred_element_type=F32,
            )
            for group in range(4):
                at = 64 + 16 * group + 8 * other
                spread[level, at : at + 8, :] = part[8 * group : 8 * group + 8]

    def place(ref, value):
        ends = jnp.zeros((TOP, LANES), value.dtype)
        for tile in range(width // LANES):
            ref[tile, 0:TOP] = ends
            ref[tile, TOP : TOP + land.shape[0]] = value[:, tile * LANES : tile * LANES + LANES]
            ref[tile, TOP + land.shape[0] :] = ends

    wet = land[...].astype(F32)
    place(ocean, wet)
    for level in range(2):
        value = kap[level] + 5.0
        place(coef.at[level], value)
        place(jacobi.at[level], wet / (value * value + 4.0))
        place(first_rhs.at[level], wet * obs[level])
        for word in range(2):
            place(word_bits.at[word, level], bits[word, level])


def corrections(gathered, spread, probe_part, even=None):
    total = gathered[0] + gathered[1] + gathered[2] + gathered[3]
    total = jnp.where(iota(total.shape, 1) >= 64, total, 0.0)
    if even is not None:
        first, last = total[:24], total[72:]
        total = jnp.concatenate(
            [jnp.where(even, first, last), total[24:72], jnp.where(even, last, first)], axis=0
        )
    for level in range(2):
        probe_part[level] = jnp.dot(total, spread[level], precision=EXACT, preferred_element_type=F32)


def first_corrections(probe_part, first_part):
    for level in range(2):
        for low, high, at in ((TOP - HALO, TOP, 16), (TOP, 40, 40), (40, 72, 64), (72, 72 + HALO, 88)):
            for tile in range(first_part.shape[1]):
                line = probe_part[level, at : at + 1, tile * LANES : tile * LANES + LANES]
                first_part[level, tile, low:high, :] = jnp.broadcast_to(line, (high - low, LANES))


def stencil(centre, above, below, other, coef, ocean):
    wide = centre.shape[1]
    beside = (above + below) + (pltpu.roll(centre, 1, 1) + pltpu.roll(centre, wide - 1, 1))
    return ocean * (coef * centre - beside - 0.5 * other)


SEGMENTS = ((TOP - HALO, TOP, 0), (TOP, 40, 1), (40, 72, 2), (72, 72 + HALO, 3))


def apply_rows(load, coef, ocean, begin, count, emit):
    for word in range(2):
        held = {}
        for step in range(2):
            for level in range(2):
                held[level, step] = load(level, word, begin - 1 + step)
        for step in range(1, count + 1):
            for level in range(2):
                held[level, step + 1] = load(level, word, begin + step)
            row = begin + step - 1
            sea = same_row(ocean, row, 0)
            for level in range(2):
                emit(
                    level,
                    word,
                    row,
                    stencil(
                        held[level, step],
                        held[level, step - 1],
                        held[level, step + 1],
                        held[1 - level, step],
                        same_row(coef.at[level], row, 0),
                        sea,
                    ),
                )


def image_kernel(
    base_ocean, base_coef, base_jacobi, base_first, base_bits,
    from_odd, from_even, gathered, spread,
    image, first_image, to_odd, to_even, own_sums, row_sums, totals, own_part,
    ocean, coef, jacobi,
    first_rhs, word_bits, direction, inner, first_direction, first_inner, probe_part, first_part,
):
    lat_at = lax.axis_index("lat")
    even = lax.rem(lax.axis_index("lon"), 2) == 0
    lat_count = lax.axis_size("lat")
    tiles, rows, _ = ocean.shape
    width = (tiles - 1) * LANES
    wide = tiles * LANES
    lon_rows = rows - 2 * TOP
    lane = iota((rows, LANES), 1)
    before = gathered[jnp.maximum(lat_at - 1, 0), 0:rows, :]
    after = gathered[jnp.minimum(lat_at + 1, lat_count - 1), 0:rows, :]
    take_before = (lane >= LANES - HALO) & (lat_at > 0)
    take_after = (lane < HALO) & (lat_at < lat_count - 1)
    odd_part, even_part = from_odd[0:32, :], from_even[0:32, :]
    prev = jnp.where(even, odd_part, even_part)
    later = jnp.where(even, even_part, odd_part)

    def outside(at):
        left = pltpu.roll(before, (LANES - HALO - 6 * at - 3) % LANES, 1)
        right = pltpu.roll(after, -6 * at % LANES, 1) if at else after
        tile = jnp.where(take_before, left, jnp.where(take_after, right, 0.0))
        here = slice(HALO * at, HALO * at + HALO)
        return prev[here], later[here], tile

    def fill(ref, base, parts):
        for tile in range(tiles - 1):
            lanes = slice(tile * LANES, tile * LANES + LANES)
            ref[tile] = base[tile]
            ref[tile, TOP - HALO : TOP] = parts[0][:, lanes]
            ref[tile, TOP + lon_rows : TOP + lon_rows + HALO] = parts[1][:, lanes]
        ref[tiles - 1] = parts[2]

    wet = outside(8)
    fill(ocean, base_ocean, wet)
    for level in range(2):
        value = [part + 5.0 for part in outside(2 + level)]
        fill(coef.at[level], base_coef.at[level], value)
        fill(
            jacobi.at[level],
            base_jacobi.at[level],
            [sea / (part * part + 4.0) for sea, part in zip(wet, value)],
        )
        fill(
            first_rhs.at[level],
            base_first.at[level],
            [sea * part for sea, part in zip(wet, outside(level))],
        )
        for word in range(2):
            fill(
                word_bits.at[word, level],
                base_bits.at[word, level],
                [part.astype(jnp.int32) for part in outside(4 + word * 2 + level)],
            )
    corrections(gathered, spread, probe_part)
    first_corrections(probe_part, first_part)
    own_part[...] = probe_part[:, 24:72, :width]
    bit = jnp.left_shift(1, iota((8, wide), 0))
    zero = jnp.zeros((8, width), F32)

    gamma = (zero, zero)
    for low, high, column in SEGMENTS:
        own = column in (1, 2)

        def body(row, carry, column=column, own=own):
            sea = same_row(ocean, row, 0)
            carry = list(carry)
            for level in range(2):
                weight = same_row(jacobi.at[level], row, 0)
                for word in range(2):
                    held = same_row(word_bits.at[word, level], row, 0)
                    rhs = jnp.where((held & bit) != 0, sea, -sea)
                    at = column * 24 + word * 8
                    value = weight * rhs + sea * probe_part[level, at : at + 8, :]
                    direction[level, word, row - (TOP - HALO)] = value
                    if own:
                        carry[word] = carry[word] + (rhs * value)[:, :width]
            return tuple(carry)

        gamma = lax.fori_loop(low, high, body, gamma, unroll=16 if own else HALO)
    first_gamma = zero
    for step in range(14):
        row = TOP - HALO + step
        sea = same_row(ocean, row, 8)
        for level in range(2):
            rhs = same_row(first_rhs.at[level], row, 8)
            value = same_row(jacobi.at[level], row, 8) * rhs + sea * same_row(first_part.at[level], row, 8)
            first_direction[level, step] = value
            if HALO <= step < HALO + 8:
                first_gamma = first_gamma + (rhs * value)[:, :width]

    def load_direction(level, word, row):
        return direction[level, word, row - (TOP - HALO)]

    def first_body(column, carry, low, count, own):
        carry = list(carry)

        def emit(level, word, row, value):
            inner[level, word, row - (TOP - HALO)] = value
            if own:
                part = value[:, :width]
                carry[word] = carry[word] + part * part

        apply_rows(load_direction, coef, ocean, low + column * count, count, emit)
        return tuple(carry)

    norm = first_body(0, (zero, zero), TOP - 2, 2, False)
    norm = lax.fori_loop(
        0, 2, functools.partial(first_body, low=TOP, count=BLK, own=True), norm
    )
    norm = first_body(0, norm, TOP + lon_rows, 2, False)
    first_norm = zero
    for step in range(1, 13):
        row = TOP - HALO + step
        sea = same_row(ocean, row, 8)
        for level in range(2):
            value = stencil(
                first_direction[level, step],
                first_direction[level, step - 1],
                first_direction[level, step + 1],
                first_direction[1 - level, step],
                same_row(coef.at[level], row, 8),
                sea,
            )
            first_inner[level, step] = value
            if HALO <= step < HALO + 8:
                part = value[:, :width]
                first_norm = first_norm + part * part

    def load_inner(level, word, row):
        return inner[level, word, row - (TOP - HALO)]

    def second_body(column, carry, low, count, own):
        added = {}

        def emit(level, word, row, value):
            image[level, word, row - (TOP - 1)] = value
            if own:
                part = value[:, :width]
                added[level, word] = added[level, word] + part if (level, word) in added else part

        apply_rows(load_inner, coef, ocean, low + column * count, count, emit)
        if own:
            for level in range(2):
                for word in range(2):
                    at = pl.multiple_of(column * 24, 8) + word * 8
                    row_sums[level, pl.ds(at, 8), :] = added[level, word]
        return carry

    second_body(0, 0, TOP - 1, 1, False)
    lax.fori_loop(0, 2, functools.partial(second_body, low=TOP, count=BLK, own=True), 0)
    second_body(0, 0, TOP + lon_rows, 1, False)
    first_sum = [zero, zero]
    for step in range(2, 12):
        row = TOP - HALO + step
        sea = same_row(ocean, row, 8)
        for level in range(2):
            value = stencil(
                first_inner[level, step],
                first_inner[level, step - 1],
                first_inner[level, step + 1],
                first_inner[1 - level, step],
                same_row(coef.at[level], row, 8),
                sea,
            )
            first_image[level, step - 2] = value
            if HALO <= step < HALO + 8:
                first_sum[level] = first_sum[level] + value[:, :width]
    for level in range(2):
        for column in range(2):
            half = first_sum[level][column * 4 : column * 4 + 4]
            row_sums[level, column * 24 + 16 : column * 24 + 24, :] = first_row(
                jnp.sum(half, axis=0, keepdims=True)
            )
    found = block_sums(lat_at, [row_sums[level] for level in range(2)])
    own_sums[...] = found
    to_odd[...] = jnp.where(even, found[:24], found[24:])
    to_even[...] = jnp.where(even, found[24:], found[:24])
    for at, value in enumerate((gamma[0], gamma[1], first_gamma, norm[0], norm[1], first_norm)):
        totals[at] = value[:, :LANES] + value[:, LANES:]


BASIS = (0, 256, 272, 288, 304, 312, 344)
PAIRS = [(first, last) for first in range(4) for last in range(first, 4)]
EDGES = (0, 31, 32, 63)


def products_kernel(
    image, first_image, ocean, coef, jacobi, base_first, base_bits,
    linear, quadratic, edge_value, edge_field, totals, basis,
    field, edge, natural,
):
    tiles, rows, _ = ocean.shape
    width = (tiles - 1) * LANES
    lon_rows = rows - 2 * TOP
    groups = lon_rows // 8
    zero = jnp.zeros((8, width), F32)
    bit = jnp.left_shift(1, iota((8, width), 0))

    def own_rows(ref):
        return jnp.concatenate(
            [ref[tile, TOP : TOP + lon_rows] for tile in range(tiles - 1)], axis=1
        )

    def put(at, value):
        for group in range(groups):
            basis[at + group] = value[8 * group : 8 * group + 8]

    whole = jnp.concatenate([ocean[tile, TOP : TOP + lon_rows] for tile in range(tiles)], axis=1)
    sea = whole[:, :width]
    up = jnp.concatenate([ocean[tile, TOP - 1 : TOP - 1 + lon_rows] for tile in range(tiles - 1)], axis=1)
    down = jnp.concatenate([ocean[tile, TOP + 1 : TOP + 1 + lon_rows] for tile in range(tiles - 1)], axis=1)
    row = iota((lon_rows, width), 0)
    first = lax.rem(row, BLK) == 0
    last = lax.rem(row, BLK) == BLK - 1
    inside = jnp.where(first | last, 0.0, 1.0)
    vertical = jnp.where(first, 0.0, up) + jnp.where(last, 0.0, down)
    across = -sea * (jnp.where(first, up, 0.0) + jnp.where(last, down, 0.0))
    left = -sea * pltpu.roll(whole, 1, 1)[:, :width]
    right = -sea * pltpu.roll(whole, tiles * LANES - 1, 1)[:, :width]
    other = -0.5 * sea
    put(BASIS[4], sea)
    selves = []
    for level in range(2):
        scale = own_rows(coef.at[level])
        put(BASIS[3] + level * groups, 0.5 / (scale * scale + 4.0))
        put(BASIS[1] + level * groups, own_rows(jacobi.at[level]) * own_rows(base_first.at[level]))
        for word in range(2):
            put(
                BASIS[5] + (word * 2 + level) * groups,
                own_rows(base_bits.at[word, level]).astype(F32),
            )
        selves.append(sea * (scale * sea - vertical))
    for at, value in enumerate(selves + [left, right, other]):
        keep(field.at[at], value * inside)
        for place, line in enumerate(EDGES):
            edge_field[place, at : at + 1, :] = value[line : line + 1]
    for place, line in enumerate(EDGES):
        edge_field[place, 5:6, :] = across[line : line + 1]
        edge_field[place, 6:8, :] = jnp.zeros((2, width), F32)
    for level in range(2):
        terms = [selves[level] * inside, left * inside, right * inside, other * inside]
        for at, (one, two) in enumerate(PAIRS):
            product = terms[one] * terms[two]
            for column in range(2):
                quadratic[level, column, at : at + 1, :] = jnp.sum(
                    product[column * BLK : column * BLK + BLK], axis=0, keepdims=True
                )

    def load(level, word, at):
        return same_row(jacobi.at[level], at, 0) * image[level, word, at - (TOP - 1)]

    def body(column, carry):
        carry = list(carry)
        sums = {}

        def emit(level, word, at, value):
            line = at - TOP
            part = value[:, :width]
            carry[2 + word] = carry[2 + word] + part * part
            edge[level, word, line] = part
            for kind, which in enumerate((level, 2, 3, 4)):
                term = part * same_row(field.at[which], line, 0)
                key = level, word, kind
                sums[key] = sums[key] + term if key in sums else term
            source = image[level, word, at - (TOP - 1)][:, :width]
            weighted = same_row(jacobi.at[level], at, 0)[:, :width] * source
            carry[word] = carry[word] + weighted * source
            held = same_row(base_bits.at[word, level], at, 0)
            basis[(level * 2 + word) * lon_rows + line] = jnp.where(
                (held & bit) != 0, weighted, -weighted
            )

        apply_rows(load, coef, ocean, TOP + column * BLK, BLK, emit)
        for (level, word, kind), value in sums.items():
            linear[level, column, word, kind] = value
        return tuple(carry)

    crossed = lax.fori_loop(0, 2, body, (zero,) * 4)
    for place, line in enumerate(EDGES):
        for level in range(2):
            for word in range(2):
                edge_value[place, level, word] = edge[level, word, line]

    first_cross, first_norm = zero, zero
    held = {}
    for level in range(2):
        for step in range(10):
            held[level, step] = same_row(jacobi.at[level], TOP - 1 + step, 8) * first_image[level, step]
    for level in range(2):
        for step in range(8):
            for tile in range(tiles - 1):
                natural[level, tile, pl.ds(step, 8, stride=8), :] = held[level, step + 1][
                    :, tile * LANES : tile * LANES + LANES
                ]
        put(
            BASIS[2] + level * groups,
            jnp.concatenate([natural[level, tile] for tile in range(tiles - 1)], axis=1),
        )
        sums = [zero] * 4
        for step in range(1, 9):
            at = TOP - 1 + step
            value = stencil(
                held[level, step],
                held[level, step - 1],
                held[level, step + 1],
                held[1 - level, step],
                same_row(coef.at[level], at, 8),
                same_row(ocean, at, 8),
            )[:, :width]
            first_norm = first_norm + value * value
            first_cross = first_cross + (held[level, step] * first_image[level, step])[:, :width]
            for kind, which in enumerate((level, 2, 3, 4)):
                sums[kind] = sums[kind] + value * same_row(field.at[which], step - 1, 8)
            if step == 1:
                edge_value[0, level, 2] = first_row(value[0:1])
                edge_value[2, level, 2] = first_row(value[4:5])
            if step == 8:
                edge_value[1, level, 2] = first_row(value[3:4])
                edge_value[3, level, 2] = first_row(value[7:8])
        for kind in range(4):
            for column in range(2):
                half = sums[kind][column * 4 : column * 4 + 4]
                linear[level, column, 2, kind] = first_row(jnp.sum(half, axis=0, keepdims=True))
    for at, value in enumerate((crossed[0], crossed[1], first_cross, crossed[2], crossed[3], first_norm)):
        totals[at] = value[:, :LANES] + value[:, LANES:]


def norms_kernel(
    gathered, spread, row_sums, linear, quadratic, edge_value, edge_field, early, late,
    packed, own_part, probe_part,
):
    even = lax.rem(lax.axis_index("lon"), 2) == 0
    corrections(gathered, spread, probe_part, even)
    wide = probe_part.shape[2]
    width = wide - LANES
    own_part[...] = probe_part[:, 24:72, :width]
    found = [early[at] for at in range(6)] + [late[at] for at in range(6)]

    def wide_row(value):
        return jnp.broadcast_to(value, (8, width))

    def own(level, column, group):
        at = column * 24 + group * 8
        return probe_part[level, at : at + 8, :]

    for level in range(2):
        for column in range(2):
            pairs = {
                pair: wide_row(quadratic[level, column, at : at + 1, :]) for at, pair in enumerate(PAIRS)
            }
            for group in range(3):
                here = own(level, column + 1, group)
                terms = [
                    here[:, :width],
                    pltpu.roll(here, 1, 1)[:, :width],
                    pltpu.roll(here, wide - 1, 1)[:, :width],
                    own(1 - level, column + 1, group)[:, :width],
                ]
                at = column * 24 + group * 8
                cross = terms[0] * row_sums[level, at : at + 8, :]
                norm = jnp.zeros((8, width), F32)
                for one in range(4):
                    inside = terms[one] * pairs[one, one]
                    double = linear[level, column, group, one]
                    for two in range(one + 1, 4):
                        double = double + terms[two] * pairs[one, two]
                    norm = norm + terms[one] * (inside + 2.0 * double)
                for place in (2 * column, 2 * column + 1):
                    beyond = (0, 2, 1, 3)[place]
                    value = edge_value[place, level, group]
                    for kind, which in enumerate((level, 2, 3, 4)):
                        value = value + terms[kind] * wide_row(edge_field[place, which : which + 1, :])
                    value = value + own(level, beyond, group)[:, :width] * wide_row(
                        edge_field[place, 5:6, :]
                    )
                    norm = norm + (value * value)
                    mine = edge_value[place, level, group]
                    norm = norm - mine * mine
                found[6 + group] = found[6 + group] + cross[:, :LANES] + cross[:, LANES:]
                found[9 + group] = found[9 + group] + norm[:, :LANES] + norm[:, LANES:]
    lane = iota((8, LANES), 1)
    probe = iota((8, LANES), 0)
    out = jnp.zeros((8, LANES), F32)
    for kind in range(4):
        for group in range(3):
            total = jnp.broadcast_to(
                jnp.sum(found[kind * 3 + group], axis=1, keepdims=True), (8, LANES)
            )
            place = lane == (64 + kind if group == 2 else (kind * 2 + group) * 8 + probe)
            out = out + jnp.where(place, total, 0.0)
    packed[...] = jnp.broadcast_to(jnp.sum(out, axis=0, keepdims=True), packed.shape)


def finish_kernel(packed, early_part, later_part, basis, solution, diagonal, residual, ocean, bits, held, sems):
    _, lon_rows, width = solution.shape
    groups = lon_rows // 8
    total = jnp.broadcast_to(jnp.sum(packed[...], axis=0, keepdims=True), (8, LANES))
    lane = iota((8, LANES), 1)
    probe = iota((8, LANES), 0)

    def get(at):
        return jnp.concatenate([basis[at + group] for group in range(groups)], axis=0)

    def send(which, level):
        target = (solution, diagonal, residual)[which]
        copy = pltpu.make_async_copy(held.at[which, level], target.at[level], sems.at[which, level])
        copy.start()
        return copy

    def weights(group):
        found = []
        for kind in range(4):
            place = lane == (64 + kind if group == 2 else (kind * 2 + group) * 8 + probe)
            found.append(
                jnp.broadcast_to(
                    jnp.sum(jnp.where(place, total, 0.0), axis=1, keepdims=True), (8, LANES)
                )
            )
        gamma, norm, cross, second = found
        ratio = cross / norm
        rest = second - ratio * cross
        alive = rest > 0.0
        later = jnp.where(alive, (norm - ratio * gamma) / jnp.where(alive, rest, 1.0), 0.0)
        earlier = gamma / norm - later * ratio
        return (
            jnp.concatenate([earlier] * (width // LANES), axis=1),
            jnp.concatenate([later] * (width // LANES), axis=1),
        )

    wet = get(BASIS[4])
    keep(ocean, wet)
    for level in range(2):
        for word in range(2):
            bits[word, level] = get(BASIS[5] + (word * 2 + level) * groups).astype(jnp.int32)
    system = [weights(group) for group in range(3)]
    bit = jnp.left_shift(1, iota((8, width), 0))
    row = iota((lon_rows, width), 0)
    share = jnp.sum(system[0][0] + system[1][0], axis=0, keepdims=True)
    share = 2.0 * wet * jnp.broadcast_to(share, (lon_rows, width))
    earlier, later = system[2][0][0:1], system[2][1][0:1]
    copies = []
    for level in range(2):
        lines = [
            earlier * early_part[level, at : at + 1, :] + later * later_part[level, at : at + 1, :]
            for at in (16, 40)
        ]
        held[0, level] = (
            earlier * get(BASIS[1] + level * groups)
            + later * get(BASIS[2] + level * groups)
            + wet * jnp.where(row < BLK, lines[0], lines[1])
        )
        copies.append(send(0, level))
    for level in range(2):
        for column in range(2):
            coarse = []
            for word in range(2):
                at = column * 24 + word * 8
                coarse.append(
                    system[word][0] * early_part[level, at : at + 8, :]
                    + system[word][1] * later_part[level, at : at + 8, :]
                )

            def body(line, carry, coarse=coarse, level=level):
                signs, rest = None, None
                for word in range(2):
                    signed = jnp.where(
                        (row_of(bits.at[word, level], line) & bit) != 0, coarse[word], -coarse[word]
                    )
                    second = system[word][1] * basis[(level * 2 + word) * lon_rows + line]
                    signs = signed if signs is None else signs + signed
                    rest = second if rest is None else rest + second
                whole = same_row(ocean, line, 0) * signs + rest
                held[1, level, pl.ds(line, 1), :] = jnp.sum(whole, axis=0, keepdims=True)
                return carry

            lax.fori_loop(column * BLK, column * BLK + BLK, body, 0, unroll=BLK)
        bound = get(BASIS[3] + level * groups)
        spread = (held[1, level] + share * bound) / PROBES
        held[1, level] = spread
        copies.append(send(1, level))
        held[2, level] = held[0, level] / jnp.maximum(spread, bound)
        copies.append(send(2, level))
    for copy in copies:
        copy.wait()


def call(kernel, outs, scratch=(), outside=0):
    return functools.partial(_run, kernel, outs, scratch, outside)


def _run(kernel, outs, scratch, outside, *args):
    held = [pltpu.with_memory_space_constraint(array, pltpu.HBM) for array in args[:outside]]
    return pl.pallas_call(
        kernel,
        out_shape=outs,
        in_specs=[pl.BlockSpec(memory_space=pltpu.HBM)] * outside + vmem(len(args) - outside),
        out_specs=tuple(vmem(len(outs))),
        scratch_shapes=list(scratch),
        compiler_params=pltpu.CompilerParams(vmem_limit_bytes=24 << 20),
    )(*held, *args[outside:])


def per_device(observed, kappa_squared, probe_bits, land_sea, coarse_block_inverse):
    lon_rows, width = land_sea.shape
    wide = width + LANES
    tiles = wide // LANES
    rows = lon_rows + 2 * TOP
    lon_count = lax.axis_size("lon")
    lat_count = lax.axis_size("lat")
    evens = [(i, i + 1 - 2 * (i % 2)) for i in range(lon_count)]
    odds = [(i, (i - 1 + 2 * (i % 2)) % lon_count) for i in range(lon_count)]
    raw = (observed, kappa_squared, probe_bits, land_sea)
    inside = [pltpu.VMEM(array.shape, array.dtype) for array in raw]
    sems = pltpu.SemaphoreType.DMA((4,))

    to_odd, to_even, own = call(
        prepare_kernel,
        (shape(48, width), shape(48, width), shape(96, LANES)),
        [*inside, pltpu.VMEM((width // LANES, lon_rows, LANES), F32), sems],
        4,
    )(*raw)
    from_odd = lax.ppermute(to_odd, "lon", odds)
    from_even = lax.ppermute(to_even, "lon", evens)
    natural = (tiles - 1, rows, LANES)
    spread, *base = call(
        base_kernel,
        (
            shape(2, LANES, wide),
            shape(*natural),
            shape(2, *natural),
            shape(2, *natural),
            shape(2, *natural),
            jax.ShapeDtypeStruct((2, 2, *natural), jnp.int32),
        ),
        [
            *inside,
            pltpu.VMEM(coarse_block_inverse.shape, F32),
            pltpu.SemaphoreType.DMA((5,)),
        ],
        5,
    )(*raw, coarse_block_inverse)
    (merged,) = call(merge_kernel, (shape(96, LANES),))(own, from_odd, from_even)
    gathered = lax.all_gather(merged, "lat")
    probe_parts = pltpu.VMEM((2, 96, wide), F32)
    first_parts = pltpu.VMEM((2, tiles, rows, LANES), F32)
    image, first_image, to_odd, to_even, own_sums, row_sums, early, own_part, ocean, coef, jacobi = call(
        image_kernel,
        (
            shape(2, 2, lon_rows + 2, 8, wide),
            shape(2, 10, 8, wide),
            shape(24, LANES),
            shape(24, LANES),
            shape(48, LANES),
            shape(2, 48, width),
            shape(6, 8, LANES),
            shape(2, 48, width),
            shape(tiles, rows, LANES),
            shape(2, tiles, rows, LANES),
            shape(2, tiles, rows, LANES),
        ),
        [
            first_parts,
            pltpu.VMEM((2, 2, tiles, rows, LANES), jnp.int32),
            pltpu.VMEM((2, 2, lon_rows + 2 * HALO, 8, wide), F32),
            pltpu.VMEM((2, 2, lon_rows + 2 * HALO, 8, wide), F32),
            pltpu.VMEM((2, 14, 8, wide), F32),
            pltpu.VMEM((2, 14, 8, wide), F32),
            probe_parts,
            first_parts,
        ],
    )(*base, from_odd, from_even, gathered, spread)

    sums_odd = lax.ppermute(to_odd, "lon", odds)
    sums_even = lax.ppermute(to_even, "lon", evens)
    blocks = width // LANES
    linear, quadratic, edge_value, edge_field, late, basis = call(
        products_kernel,
        (
            shape(2, 2, 3, 4, 8, width),
            shape(2, 2, 16, width),
            shape(4, 2, 3, 8, width),
            shape(4, 8, width),
            shape(6, 8, LANES),
            shape(BASIS[-1], 8, width),
        ),
        [
            pltpu.VMEM((5, blocks, lon_rows, LANES), F32),
            pltpu.VMEM((2, 2, lon_rows, 8, width), F32),
            pltpu.VMEM((2, blocks, lon_rows, LANES), F32),
        ],
    )(image, first_image, ocean, coef, jacobi, base[3], base[4])
    sums = lax.all_gather(jnp.concatenate([sums_odd, own_sums, sums_even], axis=0), "lat")
    packed, later_part = call(
        norms_kernel, (shape(lon_count * lat_count, LANES), shape(2, 48, width)), [probe_parts]
    )(
        sums, spread, row_sums, linear, quadratic, edge_value, edge_field, early, late
    )
    everyone = lax.all_to_all(packed, ("lon", "lat"), 0, 0)
    return tuple(
        pl.pallas_call(
            finish_kernel,
            out_shape=(shape(2, lon_rows, width),) * 3,
            in_specs=vmem(4),
            out_specs=tuple([pl.BlockSpec(memory_space=pltpu.HBM)] * 3),
            scratch_shapes=[
                pltpu.VMEM((blocks, lon_rows, LANES), F32),
                pltpu.VMEM((2, 2, lon_rows, width), jnp.int32),
                pltpu.VMEM((3, 2, lon_rows, width), F32),
                pltpu.SemaphoreType.DMA((3, 2)),
            ],
            compiler_params=pltpu.CompilerParams(vmem_limit_bytes=24 << 20),
        )(everyone, own_part, later_part, basis)
    )


def solution(mesh):
    placed = (
        P(None, "lon", "lat"),
        P(None, "lon", "lat"),
        P(None, None, "lon", "lat"),
        P("lon", "lat"),
        P(),
    )
    return jax.shard_map(
        per_device,
        mesh=mesh,
        in_specs=placed,
        out_specs=(P(None, "lon", "lat"), P(None, "lon", "lat"), P(None, "lon", "lat")),
        check_vma=False,
    )
```

time: 95.2 us -> 68.5 us (0.72)
  blocking collectives: 16.5 us -> 37.8 us
  Pallas kernels: 29.1 us -> 14.8 us
  starting transfers between devices: 25.7 us -> 13.7 us
  waiting for transfers between devices: 12.1 us -> 1.33 us
  local copies, waits for them, and re-layouts: 10.7 us -> 0 us
    all_to_all x0 -> x1, blocking collectives: none -> 20.8 us  [per_device(): everyone = lax.all_to_all(packed, ('lon', 'lat'), 0, 0)]
    pallas_call x7, Pallas kernels: 29.1 us -> 14.8 us  [the longest x6 13.2 us: _run(): pl.pallas_call(kernel, out_shape=outs, in_specs=[pl.BlockSpec(memory_spac...]
    all_to_all x1 -> x0, waiting for transfers between devices: 10.9 us -> none  [per_device(): everyone = lax.all_to_all(packed, ('lon', 'lat'), 0, 0)]
    unnamed x28 -> x0, local copies, waits for them, and re-layouts: 10.7 us -> none
    all_to_all x1 -> x0, starting transfers between devices: 9.88 us -> none  [per_device(): everyone = lax.all_to_all(packed, ('lon', 'lat'), 0, 0)]
    ppermute x4, starting transfers between devices: 15.8 us -> 13.7 us  [the longest x1 9.7 us: per_device(): from_odd = lax.ppermute(to_odd, 'lon', odds)]
  transfers between devices with their start and end apart: 5 -> 4, of which waited for: 3 -> 1; matrix products, arithmetic and copies ran while one was open for 0% -> 0% of each run, Pallas kernels for 1% -> 7%
where the time goes in v1:
time: 68.5 us; the launch traced here: 68.3 us
  blocking collectives  37.8 us (55%)
  Pallas kernels  14.8 us (22%)
  starting transfers between devices  13.7 us (20%)
  waiting for transfers between devices  1.33 us (2%)
  between operations  0.7 us (1%)
    all_to_all x1, blocking collectives, per_device(): everyone = lax.all_to_all(packed, ('lon', 'lat'), 0, 0)  20.8 us
    pallas_call x6, Pallas kernels, _run(): pl.pallas_call(kernel, out_shape=outs, in_specs=[pl.BlockSpec(memory_spac...  13.2 us
    ppermute x1, starting transfers between devices, per_device(): from_odd = lax.ppermute(to_odd, 'lon', odds)  9.7 us
    all_gather x1, blocking collectives, per_device(): gathered = lax.all_gather(merged, 'lat')  9.05 us
    all_gather x1, blocking collectives, per_device(): lax.all_gather(jnp.concatenate([sums_odd, own_sums, sums_even], axis=0),...  7.94 us
    ppermute x1, starting transfers between devices, per_device(): sums_odd = lax.ppermute(to_odd, 'lon', odds)  4.04 us
    pallas_call x1, Pallas kernels, per_device(): pl.pallas_call(finish_kernel, out_shape=(shape(2, lon_rows, width),) * 3,...  1.56 us
  transfers between devices with their start and end apart: 4, of which 1 were waited for; matrix products, arithmetic and copies ran while one was open for 0% of the time, Pallas kernels for 7%

profile of v1, /device:TPU:1, one launch (start us, length us, event | category | flops | bytes accessed | tf_op | source)
XLA Modules:
  0.0 68.3 jit_solution(6520364620568737801)
XLA Ops:
  0.6 1.8 %shard_map.77 = (f32[48,256]{1,0:T(8,128)S(1)}, f32[48,256]{1,0:T(8,128)S(1)}, f32[96,128]{1,0:T(8,128)S(1)}) custom-call(f32[2,64,256]{2,1,0:T(8,128)} %obs_in.3, f32[2,64,256]{2,1,0:T(8,128)} %kap_in.3, s32[2,2,64,256]{3,2,1,0:T(8,128)} %bits_in.3, s32[64,256]{1,0:T(8,128)} %land_in.3), custom_call_target="tpu_custom_call" | custom-call | tf_op jit(solution)/shard_map/pallas_call | solution.py:775
  2.4 9.7 %collective-permute-start = (f32[48,256]{1,0:T(8,128)S(1)}, f32[48,256]{1,0:T(8,128)S(1)}, u32[]{:S(2)}, u32[]{:S(2)}) collective-permute-start(f32[48,256]{1,0:T(8,128)S(1)} %get-tuple-element.36), channel_id=1, source_target_pairs={{0,252},{4,8},{8,4},{12,16},{16,12},{20,24},{24,20},{28,32},{32,28... | collective-permute-start | bytes 147464 | tf_op jit(solution)/shard_map/ppermute | solution.py:804
  12.1 0.0 collective-permute-start.1
  12.1 1.6 %shard_map.76 = (f32[2,128,384]{2,1,0:T(8,128)S(1)}, f32[2,80,128]{2,1,0:T(8,128)S(1)}, f32[2,2,80,128]{3,2,1,0:T(8,128)S(1)}, f32[2,2,80,128]{3,2,1,0:T(8,128)S...) custom-call(f32[2,64,256]{2,1,0:T(8,128)} %obs_in.3, f32[2,64,256]{2,1,0:T(8,128)} %kap_in.3, ...), custom_call_target="tpu_custom_call" | custom-call | tf_op jit(solution)/shard_map/pallas_call | solution.py:775
  13.7 0.0 collective-permute-done.from_odd
  13.7 1.3 %collective-permute-done.1.from_even = f32[48,256]{1,0:T(8,128)S(1)} collective-permute-done((f32[48,256]{1,0:T(8,128)S(1)}, f32[48,256]{1,0:T(8,128)S(1)}, u32[]{:S(2)}, u32[]{:S(2)}) %collective-permute-start.1) | collective-permute-done | bytes 49184 | tf_op jit(solution)/shard_map/ppermute | solution.py:805
  15.1 9.0 %all-gather = f32[384,128]{1,0:T(8,128)S(1)} all-gather(f32[96,128]{1,0:T(8,128)S(1)} %shard_map.78), channel_id=2, replica_groups=mesh['lon'=64,'lat'=4] {'lat'}, dimensions={0}, use_global_device_ids=true | all-gather | bytes 245760 | tf_op jit(solution)/shard_map/all_gather | solution.py:825
  24.1 6.1 %shard_map.79 = (f32[2,2,66,8,384]{4,3,2,1,0:T(8,128)S(1)}, f32[2,10,8,384]{3,2,1,0:T(8,128)S(1)}, f32[24,128]{1,0:T(8,128)S(1)}, f32[24,128]{1,0:T(8,128)S(1)},...) custom-call(f32[2,80,128]{2,1,0:T(8,128)S(1)} %get-tuple-element.31., ...), custom_call_target="tpu_custom_call" | custom-call | tf_op jit(solution)/shard_map/pallas_call | solution.py:775
  30.2 4.0 %collective-permute-start.2 = (f32[24,128]{1,0:T(8,128)S(1)}, f32[24,128]{1,0:T(8,128)S(1)}, u32[]{:S(2)}, u32[]{:S(2)}) collective-permute-start(f32[24,128]{1,0:T(8,128)S(1)} %get-tuple-element.40), channel_id=1, source_target_pairs={{0,252},{4,8},{8,4},{12,16},{16,12},{20,24},{24,20},{28,32},{32,28... | collective-permute-start | bytes 36872 | tf_op jit(solution)/shard_map/ppermute | solution.py:855
  34.2 0.0 collective-permute-start.3
  34.3 3.1 %shard_map.80 = (f32[2,2,3,4,8,256]{5,4,3,2,1,0:T(8,128)S(1)}, f32[2,2,16,256]{3,2,1,0:T(8,128)S(1)}, f32[4,2,3,8,256]{4,3,2,1,0:T(8,128)S(1)}, f32[4,8,256]{2,1...) custom-call(f32[2,2,66,8,384]{4,3,2,1,0:T(8,128)S(1)} %get-tuple-element.44.image, ...), custom_call_target="tpu_custom_call" | custom-call | tf_op jit(solution)/shard_map/pallas_call | solution.py:775
  37.4 0.0 collective-permute-done.2
  37.4 0.0 collective-permute-done.3
  37.4 7.9 %all-gather.1 = f32[384,128]{1,0:T(8,128)S(1)} all-gather(f32[96,128]{1,0:T(8,128)S(1)} %pad_maximum_fusion), channel_id=3, replica_groups=mesh['lon'=64,'lat'=4] {'lat'}, dimensions={0}, use_global_device_ids=true | all-gather | bytes 245760 | tf_op jit(solution)/shard_map/all_gather | solution.py:874
  45.3 0.7 shard_map.81
  46.0 20.8 %all_to_all.11 = f32[256,1,128]{2,1,0:T(1,128)S(1)} all-to-all(f32[256,1,128]{2,1,0:T(1,128)S(1)} %bitcast.9), channel_id=1, replica_groups=mesh['lon'=64,'lat'=4] {'lon','lat'}, dimensions={0} | all-to-all | bytes 262144 | tf_op jit(solution)/shard_map/all_to_all | solution.py:880
  66.8 1.6 %shard_map.82 = (f32[2,64,256]{2,1,0:T(8,128)}, f32[2,64,256]{2,1,0:T(8,128)}, f32[2,64,256]{2,1,0:T(8,128)}) custom-call(f32[256,128]{1,0:T(8,128)S(1)} %bitcast.8, f32[2,48,256]{2,1,0:T(8,128)S(1)} %get-tuple-element.56.early_part, f32[2,48,256]{2,1,0:T(8,128)S(1)} %get-tuple-element.57.later_part, f32[344,8,256]{2,1,0:T(8,128)S(1)} %get-tuple-element.58.basis), custom_call_target="tpu_custom_call" | custom-call | tf_op jit(solution)/shard_map/pallas_call | solution.py:882
  (2 shorter events, 0.0 us)
Async XLA Ops:
  2.4 11.3 %collective-permute-start = (f32[48,256]{1,0:T(8,128)S(1)}, f32[48,256]{1,0:T(8,128)S(1)}, u32[]{:S(2)}, u32[]{:S(2)}) collective-permute-start(f32[48,256]{1,0:T(8,128)S(1)} %get-tuple-element.36), channel_id=1, source_target_pairs={{0,252},{4,8},{8,4},{12,16},{16,12},{20,24},{24,20},{28,32},{32,28... | collective-permute-start | bytes 147464 | tf_op jit(solution)/shard_map/ppermute | solution.py:804
  12.1 2.9 %collective-permute-start.1 = (f32[48,256]{1,0:T(8,128)S(1)}, f32[48,256]{1,0:T(8,128)S(1)}, u32[]{:S(2)}, u32[]{:S(2)}) collective-permute-start(f32[48,256]{1,0:T(8,128)S(1)} %get-tuple-element.37), channel_id=1, source_target_pairs={{0,4},{4,0},{8,12},{12,8},{16,20},{20,16},{24,28},{28,24},{32,36},... | collective-permute-start | bytes 147464 | tf_op jit(solution)/shard_map/ppermute | solution.py:805
  30.2 7.1 %collective-permute-start.2 = (f32[24,128]{1,0:T(8,128)S(1)}, f32[24,128]{1,0:T(8,128)S(1)}, u32[]{:S(2)}, u32[]{:S(2)}) collective-permute-start(f32[24,128]{1,0:T(8,128)S(1)} %get-tuple-element.40), channel_id=1, source_target_pairs={{0,252},{4,8},{8,4},{12,16},{16,12},{20,24},{24,20},{28,32},{32,28... | collective-permute-start | bytes 36872 | tf_op jit(solution)/shard_map/ppermute | solution.py:855
  34.2 3.1 %collective-permute-start.3 = (f32[24,128]{1,0:T(8,128)S(1)}, f32[24,128]{1,0:T(8,128)S(1)}, u32[]{:S(2)}, u32[]{:S(2)}) collective-permute-start(f32[24,128]{1,0:T(8,128)S(1)} %get-tuple-element.42), channel_id=1, source_target_pairs={{0,4},{4,0},{8,12},{12,8},{16,20},{20,16},{24,28},{28,24},{32,36},... | collective-permute-start | bytes 36872 | tf_op jit(solution)/shard_map/ppermute | solution.py:856

commit v2 on v1

--- a/solution.py
+++ b/solution.py
@@ -91,7 +91,7 @@
 
 
 def prepare_kernel(
-    obs_in, kap_in, bits_in, land_in, to_odd, to_even, own,
+    obs_in, kap_in, bits_in, land_in, to_odd, to_even, own, rhs_sums,
     obs, kap, bits, land, ocean, sems,
 ):
     fetch((obs_in, kap_in, bits_in, land_in), (obs, kap, bits, land), sems)
@@ -144,6 +144,8 @@
         for level in range(2)
     ]
     found = block_sums(lat_at, rows)
+    for level in range(2):
+        rhs_sums[level] = rows[level]
     own[...] = jnp.zeros(own.shape, F32)
     own[TOP : TOP + lon_rows, :] = edges
     own[24:72, :] = own[24:72, :] + found
@@ -171,7 +173,8 @@
 
 
 def base_kernel(
-    obs_in, kap_in, bits_in, land_in, coarse_in, spread, ocean, coef, jacobi, first_rhs, word_bits,
+    obs_in, kap_in, bits_in, land_in, coarse_in,
+    spread, ocean, coef, jacobi, first_rhs, word_bits, begin,
     obs, kap, bits, land, coarse, sems,
 ):
     fetch(
@@ -216,6 +219,17 @@
         place(first_rhs.at[level], wet * obs[level])
         for word in range(2):
             place(word_bits.at[word, level], bits[word, level])
+    bit = jnp.left_shift(1, iota((8, width), 0))
+
+    def body(row, carry):
+        for level in range(2):
+            weight = same_row(jacobi.at[level], TOP + row, 0)
+            for word in range(2):
+                held = row_of(bits.at[word, level], row)
+                begin[level, word, row] = jnp.where((held & bit) != 0, weight, -weight)
+        return carry
+
+    lax.fori_loop(0, land.shape[0], body, 0, unroll=16)
 
 
 def corrections(gathered, spread, probe_part, even=None):
@@ -275,7 +289,7 @@
 
 
 def image_kernel(
-    base_ocean, base_coef, base_jacobi, base_first, base_bits,
+    base_ocean, base_coef, base_jacobi, base_first, base_bits, begin,
     from_odd, from_even, gathered, spread,
     image, first_image, to_odd, to_even, own_sums, row_sums, totals, own_part,
     ocean, coef, jacobi,
@@ -339,26 +353,30 @@
     bit = jnp.left_shift(1, iota((8, wide), 0))
     zero = jnp.zeros((8, width), F32)
 
-    gamma = (zero, zero)
     for low, high, column in SEGMENTS:
         own = column in (1, 2)
 
         def body(row, carry, column=column, own=own):
             sea = same_row(ocean, row, 0)
-            carry = list(carry)
             for level in range(2):
                 weight = same_row(jacobi.at[level], row, 0)
                 for word in range(2):
-                    held = same_row(word_bits.at[word, level], row, 0)
-                    rhs = jnp.where((held & bit) != 0, sea, -sea)
+                    if own:
+                        place = pl.ds(row, 8, stride=0)
+                        part = jacobi[level, tiles - 1, place, :]
+                        held = word_bits[word, level, tiles - 1, place, :]
+                        part = jnp.where((held & bit[:, :LANES]) != 0, part, -part)
+                        fine = jnp.concatenate([begin[level, word, row - TOP], part], axis=1)
+                    else:
+                        held = same_row(word_bits.at[word, level], row, 0)
+                        fine = jnp.where((held & bit) != 0, weight, -weight)
                     at = column * 24 + word * 8
-                    value = weight * rhs + sea * probe_part[level, at : at + 8, :]
-                    direction[level, word, row - (TOP - HALO)] = value
-                    if own:
-                        carry[word] = carry[word] + (rhs * value)[:, :width]
-            return tuple(carry)
-
-        gamma = lax.fori_loop(low, high, body, gamma, unroll=16 if own else HALO)
+                    direction[level, word, row - (TOP - HALO)] = (
+                        fine + sea * probe_part[level, at : at + 8, :]
+                    )
+            return carry
+
+        lax.fori_loop(low, high, body, 0, unroll=BLK if own else HALO)
     first_gamma = zero
     for step in range(14):
         row = TOP - HALO + step
@@ -373,23 +391,16 @@
     def load_direction(level, word, row):
         return direction[level, word, row - (TOP - HALO)]
 
-    def first_body(column, carry, low, count, own):
-        carry = list(carry)
-
+    def first_body(column, carry, low, count):
         def emit(level, word, row, value):
             inner[level, word, row - (TOP - HALO)] = value
-            if own:
-                part = value[:, :width]
-                carry[word] = carry[word] + part * part
 
         apply_rows(load_direction, coef, ocean, low + column * count, count, emit)
-        return tuple(carry)
-
-    norm = first_body(0, (zero, zero), TOP - 2, 2, False)
-    norm = lax.fori_loop(
-        0, 2, functools.partial(first_body, low=TOP, count=BLK, own=True), norm
-    )
-    norm = first_body(0, norm, TOP + lon_rows, 2, False)
+        return carry
+
+    first_body(0, 0, TOP - 2, 2)
+    lax.fori_loop(0, 2, functools.partial(first_body, low=TOP, count=BLK), 0, unroll=2)
+    first_body(0, 0, TOP + lon_rows, 2)
     first_norm = zero
     for step in range(1, 13):
         row = TOP - HALO + step
@@ -429,7 +440,7 @@
         return carry
 
     second_body(0, 0, TOP - 1, 1, False)
-    lax.fori_loop(0, 2, functools.partial(second_body, low=TOP, count=BLK, own=True), 0)
+    lax.fori_loop(0, 2, functools.partial(second_body, low=TOP, count=BLK, own=True), 0, unroll=2)
     second_body(0, 0, TOP + lon_rows, 1, False)
     first_sum = [zero, zero]
     for step in range(2, 12):
@@ -457,7 +468,7 @@
     own_sums[...] = found
     to_odd[...] = jnp.where(even, found[:24], found[24:])
     to_even[...] = jnp.where(even, found[24:], found[:24])
-    for at, value in enumerate((gamma[0], gamma[1], first_gamma, norm[0], norm[1], first_norm)):
+    for at, value in enumerate((first_gamma, first_norm)):
         totals[at] = value[:, :LANES] + value[:, LANES:]
 
 
@@ -467,7 +478,7 @@
 
 
 def products_kernel(
-    image, first_image, ocean, coef, jacobi, base_first, base_bits,
+    image, first_image, ocean, coef, jacobi, base_first, base_bits, own_part, rhs_sums, row_sums,
     linear, quadratic, edge_value, edge_field, totals, basis,
     field, edge, natural,
 ):
@@ -548,16 +559,16 @@
             weighted = same_row(jacobi.at[level], at, 0)[:, :width] * source
             carry[word] = carry[word] + weighted * source
             held = same_row(base_bits.at[word, level], at, 0)
-            basis[(level * 2 + word) * lon_rows + line] = jnp.where(
-                (held & bit) != 0, weighted, -weighted
-            )
+            signed = jnp.where((held & bit) != 0, weighted, -weighted)
+            carry[4 + word] = carry[4 + word] + signed
+            basis[(level * 2 + word) * lon_rows + line] = signed
 
         apply_rows(load, coef, ocean, TOP + column * BLK, BLK, emit)
         for (level, word, kind), value in sums.items():
             linear[level, column, word, kind] = value
         return tuple(carry)
 
-    crossed = lax.fori_loop(0, 2, body, (zero,) * 4)
+    crossed = lax.fori_loop(0, 2, body, (zero,) * 6)
     for place, line in enumerate(EDGES):
         for level in range(2):
             for word in range(2):
@@ -603,7 +614,21 @@
             for column in range(2):
                 half = sums[kind][column * 4 : column * 4 + 4]
                 linear[level, column, 2, kind] = first_row(jnp.sum(half, axis=0, keepdims=True))
-    for at, value in enumerate((crossed[0], crossed[1], first_cross, crossed[2], crossed[3], first_norm)):
+    weight_sum = sum(
+        jnp.sum(own_rows(jacobi.at[level]), axis=0, keepdims=True) for level in range(2)
+    )
+    gamma, norm = [], []
+    for word in range(2):
+        gamma.append(jnp.broadcast_to(weight_sum, (8, width)))
+        norm.append(crossed[4 + word])
+        for level in range(2):
+            for column in range(2):
+                here = slice(column * 24 + word * 8, column * 24 + word * 8 + 8)
+                gamma[word] = gamma[word] + own_part[level, here] * rhs_sums[level, here]
+                norm[word] = norm[word] + own_part[level, here] * row_sums[level, here]
+    for at, value in enumerate(
+        (crossed[0], crossed[1], first_cross, crossed[2], crossed[3], first_norm, *gamma, *norm)
+    ):
         totals[at] = value[:, :LANES] + value[:, LANES:]
 
 
@@ -616,7 +641,7 @@
     wide = probe_part.shape[2]
     width = wide - LANES
     own_part[...] = probe_part[:, 24:72, :width]
-    found = [early[at] for at in range(6)] + [late[at] for at in range(6)]
+    found = [late[6], late[7], early[0], late[8], late[9], early[1]] + [late[at] for at in range(6)]
 
     def wide_row(value):
         return jnp.broadcast_to(value, (8, width))
@@ -795,9 +820,9 @@
     inside = [pltpu.VMEM(array.shape, array.dtype) for array in raw]
     sems = pltpu.SemaphoreType.DMA((4,))
 
-    to_odd, to_even, own = call(
+    to_odd, to_even, own, rhs_sums = call(
         prepare_kernel,
-        (shape(48, width), shape(48, width), shape(96, LANES)),
+        (shape(48, width), shape(48, width), shape(96, LANES), shape(2, 48, width)),
         [*inside, pltpu.VMEM((width // LANES, lon_rows, LANES), F32), sems],
         4,
     )(*raw)
@@ -813,6 +838,7 @@
             shape(2, *natural),
             shape(2, *natural),
             jax.ShapeDtypeStruct((2, 2, *natural), jnp.int32),
+            shape(2, 2, lon_rows, 8, width),
         ),
         [
             *inside,
@@ -834,7 +860,7 @@
             shape(24, LANES),
             shape(48, LANES),
             shape(2, 48, width),
-            shape(6, 8, LANES),
+            shape(2, 8, LANES),
             shape(2, 48, width),
             shape(tiles, rows, LANES),
             shape(2, tiles, rows, LANES),
@@ -862,7 +888,7 @@
             shape(2, 2, 16, width),
             shape(4, 2, 3, 8, width),
             shape(4, 8, width),
-            shape(6, 8, LANES),
+            shape(10, 8, LANES),
             shape(BASIS[-1], 8, width),
         ),
         [
@@ -870,7 +896,7 @@
             pltpu.VMEM((2, 2, lon_rows, 8, width), F32),
             pltpu.VMEM((2, blocks, lon_rows, LANES), F32),
         ],
-    )(image, first_image, ocean, coef, jacobi, base[3], base[4])
+    )(image, first_image, ocean, coef, jacobi, base[3], base[4], own_part, rhs_sums, row_sums)
     sums = lax.all_gather(jnp.concatenate([sums_odd, own_sums, sums_even], axis=0), "lat")
     packed, later_part = call(
         norms_kernel, (shape(lon_count * lat_count, LANES), shape(2, 48, width)), [probe_parts]

time: 68.5 us -> 67.5 us (0.985)
  transfers between devices with their start and end apart: 4 -> 4, of which waited for: 1 -> 1; matrix products, arithmetic and copies ran while one was open for 0% -> 0% of each run, Pallas kernels for 7% -> 8%
where the time goes in v2:
time: 67.5 us; the launch traced here: 67.4 us
  blocking collectives  37.6 us (56%)
  Pallas kernels  14.3 us (21%)
  starting transfers between devices  13.7 us (20%)
  waiting for transfers between devices  1.02 us (2%)
  between operations  0.7 us (1%)
    all_to_all x1, blocking collectives, per_device(): everyone = lax.all_to_all(packed, ('lon', 'lat'), 0, 0)  20.8 us
    pallas_call x6, Pallas kernels, _run(): pl.pallas_call(kernel, out_shape=outs, in_specs=[pl.BlockSpec(memory_spac...  12.7 us
    ppermute x1, starting transfers between devices, per_device(): from_odd = lax.ppermute(to_odd, 'lon', odds)  9.7 us
    all_gather x1, blocking collectives, per_device(): gathered = lax.all_gather(merged, 'lat')  9.04 us
    all_gather x1, blocking collectives, per_device(): lax.all_gather(jnp.concatenate([sums_odd, own_sums, sums_even], axis=0),...  7.81 us
    ppermute x1, starting transfers between devices, per_device(): sums_odd = lax.ppermute(to_odd, 'lon', odds)  4.04 us
    pallas_call x1, Pallas kernels, per_device(): pl.pallas_call(finish_kernel, out_shape=(shape(2, lon_rows, width),) * 3,...  1.56 us
  transfers between devices with their start and end apart: 4, of which 1 were waited for; matrix products, arithmetic and copies ran while one was open for 0% of the time, Pallas kernels for 8%

profile of v2, /device:TPU:1, one launch (start us, length us, event | category | flops | bytes accessed | tf_op | source)
XLA Modules:
  0.0 67.4 jit_solution(12982851573666379429)
XLA Ops:
  0.6 1.8 %shard_map.77 = (f32[48,256]{1,0:T(8,128)S(1)}, f32[48,256]{1,0:T(8,128)S(1)}, f32[96,128]{1,0:T(8,128)S(1)}, f32[2,48,256]{2,1,0:T(8,128)S(1)}) custom-call(f32[2,64,256]{2,1,0:T(8,128)} %obs_in.3, f32[2,64,256]{2,1,0:T(8,128)} %kap_in.3, s32[2,2,64,256]{3,2,1,0:T(8,128)} %bits_in.3, s32[64,256]{1,0:T(8,128)} %land_in.3), custom_call_target="tpu_custom_call" | custom-call | tf_op jit(solution)/shard_map/pallas_call | solution.py:800
  2.4 9.7 %collective-permute-start = (f32[48,256]{1,0:T(8,128)S(1)}, f32[48,256]{1,0:T(8,128)S(1)}, u32[]{:S(2)}, u32[]{:S(2)}) collective-permute-start(f32[48,256]{1,0:T(8,128)S(1)} %get-tuple-element.39), channel_id=1, source_target_pairs={{0,252},{4,8},{8,4},{12,16},{16,12},{20,24},{24,20},{28,32},{32,28... | collective-permute-start | bytes 147464 | tf_op jit(solution)/shard_map/ppermute | solution.py:829
  12.1 0.0 collective-permute-start.1
  12.1 1.9 %shard_map.76 = (f32[2,128,384]{2,1,0:T(8,128)S(1)}, f32[2,80,128]{2,1,0:T(8,128)S(1)}, f32[2,2,80,128]{3,2,1,0:T(8,128)S(1)}, f32[2,2,80,128]{3,2,1,0:T(8,128)S...) custom-call(f32[2,64,256]{2,1,0:T(8,128)} %obs_in.3, ...), custom_call_target="tpu_custom_call" | custom-call | tf_op jit(solution)/shard_map/pallas_call | solution.py:800
  14.0 0.0 collective-permute-done.from_odd
  14.1 1.0 %collective-permute-done.1.from_even = f32[48,256]{1,0:T(8,128)S(1)} collective-permute-done((f32[48,256]{1,0:T(8,128)S(1)}, f32[48,256]{1,0:T(8,128)S(1)}, u32[]{:S(2)}, u32[]{:S(2)}) %collective-permute-start.1) | collective-permute-done | bytes 49184 | tf_op jit(solution)/shard_map/ppermute | solution.py:830
  15.1 9.0 %all-gather = f32[384,128]{1,0:T(8,128)S(1)} all-gather(f32[96,128]{1,0:T(8,128)S(1)} %shard_map.78), channel_id=2, replica_groups=mesh['lon'=64,'lat'=4] {'lat'}, dimensions={0}, use_global_device_ids=true | all-gather | bytes 245760 | tf_op jit(solution)/shard_map/all_gather | solution.py:851
  24.1 5.1 %shard_map.79 = (f32[2,2,66,8,384]{4,3,2,1,0:T(8,128)S(1)}, f32[2,10,8,384]{3,2,1,0:T(8,128)S(1)}, f32[24,128]{1,0:T(8,128)S(1)}, f32[24,128]{1,0:T(8,128)S(1)},...) custom-call(f32[2,80,128]{2,1,0:T(8,128)S(1)} %get-tuple-element.33., ...), custom_call_target="tpu_custom_call" | custom-call | tf_op jit(solution)/shard_map/pallas_call | solution.py:800
  29.2 4.0 %collective-permute-start.2 = (f32[24,128]{1,0:T(8,128)S(1)}, f32[24,128]{1,0:T(8,128)S(1)}, u32[]{:S(2)}, u32[]{:S(2)}) collective-permute-start(f32[24,128]{1,0:T(8,128)S(1)} %get-tuple-element.43), channel_id=1, source_target_pairs={{0,252},{4,8},{8,4},{12,16},{16,12},{20,24},{24,20},{28,32},{32,28... | collective-permute-start | bytes 36872 | tf_op jit(solution)/shard_map/ppermute | solution.py:881
  33.3 0.0 collective-permute-start.3
  33.3 3.2 %shard_map.80 = (f32[2,2,3,4,8,256]{5,4,3,2,1,0:T(8,128)S(1)}, f32[2,2,16,256]{3,2,1,0:T(8,128)S(1)}, f32[4,2,3,8,256]{4,3,2,1,0:T(8,128)S(1)}, f32[4,8,256]{2,1...) custom-call(f32[2,2,66,8,384]{4,3,2,1,0:T(8,128)S(1)} %get-tuple-element.47.image, ...), custom_call_target="tpu_custom_call" | custom-call | tf_op jit(solution)/shard_map/pallas_call | solution.py:800
  36.5 0.0 collective-permute-done.2
  36.5 0.0 collective-permute-done.3
  36.6 7.8 %all-gather.1 = f32[384,128]{1,0:T(8,128)S(1)} all-gather(f32[96,128]{1,0:T(8,128)S(1)} %pad_maximum_fusion), channel_id=3, replica_groups=mesh['lon'=64,'lat'=4] {'lat'}, dimensions={0}, use_global_device_ids=true | all-gather | bytes 245760 | tf_op jit(solution)/shard_map/all_gather | solution.py:900
  44.4 0.7 shard_map.81
  45.0 20.8 %all_to_all.11 = f32[256,1,128]{2,1,0:T(1,128)S(1)} all-to-all(f32[256,1,128]{2,1,0:T(1,128)S(1)} %bitcast.9), channel_id=1, replica_groups=mesh['lon'=64,'lat'=4] {'lon','lat'}, dimensions={0} | all-to-all | bytes 262144 | tf_op jit(solution)/shard_map/all_to_all | solution.py:906
  65.8 1.6 %shard_map.82 = (f32[2,64,256]{2,1,0:T(8,128)}, f32[2,64,256]{2,1,0:T(8,128)}, f32[2,64,256]{2,1,0:T(8,128)}) custom-call(f32[256,128]{1,0:T(8,128)S(1)} %bitcast.8, f32[2,48,256]{2,1,0:T(8,128)S(1)} %get-tuple-element.52.own_part.early_part, f32[2,48,256]{2,1,0:T(8,128)S(1)} %get-tuple-element.61.later_part, f32[344,8,256]{2,1,0:T(8,128)S(1)} %get-tuple-element.62.basis), custom_call_target="tpu_custom_call" | custom-call | tf_op jit(solution)/shard_map/pallas_call | solution.py:908
  (2 shorter events, 0.0 us)
Async XLA Ops:
  2.4 11.6 %collective-permute-start = (f32[48,256]{1,0:T(8,128)S(1)}, f32[48,256]{1,0:T(8,128)S(1)}, u32[]{:S(2)}, u32[]{:S(2)}) collective-permute-start(f32[48,256]{1,0:T(8,128)S(1)} %get-tuple-element.39), channel_id=1, source_target_pairs={{0,252},{4,8},{8,4},{12,16},{16,12},{20,24},{24,20},{28,32},{32,28... | collective-permute-start | bytes 147464 | tf_op jit(solution)/shard_map/ppermute | solution.py:829
  12.1 2.9 %collective-permute-start.1 = (f32[48,256]{1,0:T(8,128)S(1)}, f32[48,256]{1,0:T(8,128)S(1)}, u32[]{:S(2)}, u32[]{:S(2)}) collective-permute-start(f32[48,256]{1,0:T(8,128)S(1)} %get-tuple-element.40), channel_id=1, source_target_pairs={{0,4},{4,0},{8,12},{12,8},{16,20},{20,16},{24,28},{28,24},{32,36},... | collective-permute-start | bytes 147464 | tf_op jit(solution)/shard_map/ppermute | solution.py:830
  29.2 7.3 %collective-permute-start.2 = (f32[24,128]{1,0:T(8,128)S(1)}, f32[24,128]{1,0:T(8,128)S(1)}, u32[]{:S(2)}, u32[]{:S(2)}) collective-permute-start(f32[24,128]{1,0:T(8,128)S(1)} %get-tuple-element.43), channel_id=1, source_target_pairs={{0,252},{4,8},{8,4},{12,16},{16,12},{20,24},{24,20},{28,32},{32,28... | collective-permute-start | bytes 36872 | tf_op jit(solution)/shard_map/ppermute | solution.py:881
  33.3 3.3 %collective-permute-start.3 = (f32[24,128]{1,0:T(8,128)S(1)}, f32[24,128]{1,0:T(8,128)S(1)}, u32[]{:S(2)}, u32[]{:S(2)}) collective-permute-start(f32[24,128]{1,0:T(8,128)S(1)} %get-tuple-element.45), channel_id=1, source_target_pairs={{0,4},{4,0},{8,12},{12,8},{16,20},{20,16},{24,28},{28,24},{32,36},... | collective-permute-start | bytes 36872 | tf_op jit(solution)/shard_map/ppermute | solution.py:882

commit v3 on v2

--- a/solution.py
+++ b/solution.py
@@ -94,10 +94,40 @@
     obs_in, kap_in, bits_in, land_in, to_odd, to_even, own, rhs_sums,
     obs, kap, bits, land, ocean, sems,
 ):
-    fetch((obs_in, kap_in, bits_in, land_in), (obs, kap, bits, land), sems)
+    copies = [
+        pltpu.make_async_copy(source, target, sems.at[at])
+        for at, (source, target) in enumerate(
+            ((land_in, land), (bits_in, bits), (obs_in, obs), (kap_in, kap))
+        )
+    ]
+    for copy in copies:
+        copy.start()
     lat_at = lax.axis_index("lat")
     even = lax.rem(lax.axis_index("lon"), 2) == 0
     lon_rows, width = land.shape
+    copies[0].wait()
+    copies[1].wait()
+    keep(ocean, land[...].astype(F32))
+    bit = jnp.left_shift(1, iota((8, width), 0))
+    zero = jnp.zeros((8, width), F32)
+    sums = {}
+    for column in range(2):
+
+        def body(row, carry):
+            wet = same_row(ocean, row, 0)
+            out = []
+            for word in range(2):
+                for level in range(2):
+                    held = row_of(bits.at[word, level], row)
+                    out.append(carry[word * 2 + level] + jnp.where((held & bit) != 0, wet, -wet))
+            return tuple(out)
+
+        got = lax.fori_loop(column * BLK, column * BLK + BLK, body, (zero,) * 4, unroll=BLK)
+        for word in range(2):
+            for level in range(2):
+                sums[column, word, level] = got[word * 2 + level]
+    copies[2].wait()
+    copies[3].wait()
     fields = raw_fields(obs, kap, bits, land)
     lane = iota((lon_rows, LANES), 1)
     edges = jnp.zeros((lon_rows, LANES), F32)
@@ -112,28 +142,7 @@
         edges = jnp.where((lane >= 6 * at + 3) & (lane < 6 * at + 6), high, edges)
     to_odd[27:30, :LANES] = jnp.where(even, edges[:HALO], edges[lon_rows - HALO :])
     to_even[27:30, :LANES] = jnp.where(even, edges[lon_rows - HALO :], edges[:HALO])
-    keep(ocean, fields[8])
-    bit = jnp.left_shift(1, iota((8, width), 0))
-    zero = jnp.zeros((8, width), F32)
-    sums = {}
     for column in range(2):
-        for word in range(2):
-            for level in range(2):
-                sums[column, word, level] = zero
-
-        def body(row, carry):
-            wet = same_row(ocean, row, 0)
-            out = []
-            for word in range(2):
-                for level in range(2):
-                    held = row_of(bits.at[word, level], row)
-                    out.append(carry[word * 2 + level] + jnp.where((held & bit) != 0, wet, -wet))
-            return tuple(out)
-
-        got = lax.fori_loop(column * BLK, column * BLK + BLK, body, (zero,) * 4, unroll=BLK)
-        for word in range(2):
-            for level in range(2):
-                sums[column, word, level] = got[word * 2 + level]
         for level in range(2):
             held = slice(column * BLK, column * BLK + BLK)
             sums[column, 2, level] = first_row(
@@ -234,11 +243,15 @@
 
 def corrections(gathered, spread, probe_part, even=None):
     total = gathered[0] + gathered[1] + gathered[2] + gathered[3]
-    total = jnp.where(iota(total.shape, 1) >= 64, total, 0.0)
-    if even is not None:
-        first, last = total[:24], total[72:]
+    high = iota(total.shape, 1) >= 64
+    received = jnp.where(high, total, 0.0)
+    if even is None:
+        total = received
+    else:
+        own = jnp.where(high, pltpu.roll(total, 64, 1), 0.0)
+        first, last = received[:24], received[24:]
         total = jnp.concatenate(
-            [jnp.where(even, first, last), total[24:72], jnp.where(even, last, first)], axis=0
+            [jnp.where(even, first, last), own, jnp.where(even, last, first)], axis=0
         )
     for level in range(2):
         probe_part[level] = jnp.dot(total, spread[level], precision=EXACT, preferred_element_type=F32)
@@ -465,7 +478,7 @@
                 jnp.sum(half, axis=0, keepdims=True)
             )
     found = block_sums(lat_at, [row_sums[level] for level in range(2)])
-    own_sums[...] = found
+    own_sums[...] = pltpu.roll(found, 64, 1)
     to_odd[...] = jnp.where(even, found[:24], found[24:])
     to_even[...] = jnp.where(even, found[24:], found[:24])
     for at, value in enumerate((first_gamma, first_norm)):
@@ -897,7 +910,7 @@
             pltpu.VMEM((2, blocks, lon_rows, LANES), F32),
         ],
     )(image, first_image, ocean, coef, jacobi, base[3], base[4], own_part, rhs_sums, row_sums)
-    sums = lax.all_gather(jnp.concatenate([sums_odd, own_sums, sums_even], axis=0), "lat")
+    sums = lax.all_gather(jnp.concatenate([sums_odd + own_sums[:24], sums_even + own_sums[24:]], axis=0), "lat")
     packed, later_part = call(
         norms_kernel, (shape(lon_count * lat_count, LANES), shape(2, 48, width)), [probe_parts]
     )(

time: 67.5 us -> 67.2 us (level)
  no operation moved by 1% of the time
where the time goes in v3:
time: 67.2 us; the launch traced here: 67.1 us
  blocking collectives  37.4 us (56%)
  Pallas kernels  14.3 us (21%)
  starting transfers between devices  13.7 us (20%)
  waiting for transfers between devices  1.03 us (2%)
  between operations  0.7 us (1%)
    all_to_all x1, blocking collectives, per_device(): everyone = lax.all_to_all(packed, ('lon', 'lat'), 0, 0)  20.8 us
    pallas_call x6, Pallas kernels, _run(): pl.pallas_call(kernel, out_shape=outs, in_specs=[pl.BlockSpec(memory_spac...  12.7 us
    ppermute x1, starting transfers between devices, per_device(): from_odd = lax.ppermute(to_odd, 'lon', odds)  9.7 us
    all_gather x1, blocking collectives, per_device(): gathered = lax.all_gather(merged, 'lat')  9.05 us
    all_gather x1, blocking collectives, per_device(): lax.all_gather(jnp.concatenate([sums_odd + own_sums[:24], sums_even + own...  7.53 us
    ppermute x1, starting transfers between devices, per_device(): sums_odd = lax.ppermute(to_odd, 'lon', odds)  3.98 us
    pallas_call x1, Pallas kernels, per_device(): pl.pallas_call(finish_kernel, out_shape=(shape(2, lon_rows, width),) * 3,...  1.56 us
  transfers between devices with their start and end apart: 4, of which 1 were waited for; matrix products, arithmetic and copies ran while one was open for 0% of the time, Pallas kernels for 8%

profile of v3, /device:TPU:1, one launch (start us, length us, event | category | flops | bytes accessed | tf_op | source)
XLA Modules:
  0.0 67.1 jit_solution(5414676998003926295)
XLA Ops:
  0.6 1.6 %shard_map.77 = (f32[48,256]{1,0:T(8,128)S(1)}, f32[48,256]{1,0:T(8,128)S(1)}, f32[96,128]{1,0:T(8,128)S(1)}, f32[2,48,256]{2,1,0:T(8,128)S(1)}) custom-call(f32[2,64,256]{2,1,0:T(8,128)} %obs_in.3, f32[2,64,256]{2,1,0:T(8,128)} %kap_in.3, s32[2,2,64,256]{3,2,1,0:T(8,128)} %bits_in.3, s32[64,256]{1,0:T(8,128)} %land_in.3), custom_call_target="tpu_custom_call" | custom-call | tf_op jit(solution)/shard_map/pallas_call | solution.py:813
  2.3 9.7 %collective-permute-start = (f32[48,256]{1,0:T(8,128)S(1)}, f32[48,256]{1,0:T(8,128)S(1)}, u32[]{:S(2)}, u32[]{:S(2)}) collective-permute-start(f32[48,256]{1,0:T(8,128)S(1)} %get-tuple-element.39), channel_id=1, source_target_pairs={{0,252},{4,8},{8,4},{12,16},{16,12},{20,24},{24,20},{28,32},{32,28... | collective-permute-start | bytes 147464 | tf_op jit(solution)/shard_map/ppermute | solution.py:842
  12.0 0.0 collective-permute-start.1
  12.0 1.9 %shard_map.76 = (f32[2,128,384]{2,1,0:T(8,128)S(1)}, f32[2,80,128]{2,1,0:T(8,128)S(1)}, f32[2,2,80,128]{3,2,1,0:T(8,128)S(1)}, f32[2,2,80,128]{3,2,1,0:T(8,128)S...) custom-call(f32[2,64,256]{2,1,0:T(8,128)} %obs_in.3, ...), custom_call_target="tpu_custom_call" | custom-call | tf_op jit(solution)/shard_map/pallas_call | solution.py:813
  13.9 0.0 collective-permute-done.from_odd
  13.9 1.0 %collective-permute-done.1.from_even = f32[48,256]{1,0:T(8,128)S(1)} collective-permute-done((f32[48,256]{1,0:T(8,128)S(1)}, f32[48,256]{1,0:T(8,128)S(1)}, u32[]{:S(2)}, u32[]{:S(2)}) %collective-permute-start.1) | collective-permute-done | bytes 49184 | tf_op jit(solution)/shard_map/ppermute | solution.py:843
  14.9 9.0 %all-gather = f32[384,128]{1,0:T(8,128)S(1)} all-gather(f32[96,128]{1,0:T(8,128)S(1)} %shard_map.78), channel_id=2, replica_groups=mesh['lon'=64,'lat'=4] {'lat'}, dimensions={0}, use_global_device_ids=true | all-gather | bytes 245760 | tf_op jit(solution)/shard_map/all_gather | solution.py:864
  24.0 5.2 %shard_map.79 = (f32[2,2,66,8,384]{4,3,2,1,0:T(8,128)S(1)}, f32[2,10,8,384]{3,2,1,0:T(8,128)S(1)}, f32[24,128]{1,0:T(8,128)S(1)}, f32[24,128]{1,0:T(8,128)S(1)},...) custom-call(f32[2,80,128]{2,1,0:T(8,128)S(1)} %get-tuple-element.33., ...), custom_call_target="tpu_custom_call" | custom-call | tf_op jit(solution)/shard_map/pallas_call | solution.py:813
  29.2 4.0 %collective-permute-start.2 = (f32[24,128]{1,0:T(8,128)S(1)}, f32[24,128]{1,0:T(8,128)S(1)}, u32[]{:S(2)}, u32[]{:S(2)}) collective-permute-start(f32[24,128]{1,0:T(8,128)S(1)} %get-tuple-element.43), channel_id=1, source_target_pairs={{0,252},{4,8},{8,4},{12,16},{16,12},{20,24},{24,20},{28,32},{32,28... | collective-permute-start | bytes 36872 | tf_op jit(solution)/shard_map/ppermute | solution.py:894
  33.2 0.0 collective-permute-start.3
  33.2 3.2 %shard_map.80 = (f32[2,2,3,4,8,256]{5,4,3,2,1,0:T(8,128)S(1)}, f32[2,2,16,256]{3,2,1,0:T(8,128)S(1)}, f32[4,2,3,8,256]{4,3,2,1,0:T(8,128)S(1)}, f32[4,8,256]{2,1...) custom-call(f32[2,2,66,8,384]{4,3,2,1,0:T(8,128)S(1)} %get-tuple-element.47.image, ...), custom_call_target="tpu_custom_call" | custom-call | tf_op jit(solution)/shard_map/pallas_call | solution.py:813
  36.4 0.0 collective-permute-done.2
  36.4 0.0 collective-permute-done.3
  36.5 7.5 %all-gather.1 = f32[192,128]{1,0:T(8,128)S(1)} all-gather(f32[48,128]{1,0:T(8,128)S(1)} %pad_maximum_fusion), channel_id=3, replica_groups=mesh['lon'=64,'lat'=4] {'lat'}, dimensions={0}, use_global_device_ids=true | all-gather | bytes 122880 | tf_op jit(solution)/shard_map/all_gather | solution.py:913
  44.0 0.7 %shard_map.81 = (f32[256,128]{1,0:T(8,128)S(1)}, f32[2,48,256]{2,1,0:T(8,128)S(1)}) custom-call(f32[4,48,128]{2,1,0:T(8,128)S(1)} %bitcast.8, f32[2,128,384]{2,1,0:T(8,128)S(1)} %get-tuple-element.42.spread, f32[2,48,256]{2,1,0:T(8,128)S(1)} %get-tuple-element.46.row_sums, f32[2,2,3,4,8,256]{5,4,3,2,1,0:T(8,128)S(1)} %get-tuple-element.54.linear, ...), custom_call_target="tpu_custom_call" | custom-call | tf_op jit(solution)/shard_map/pallas_call | solution.py:813
  44.7 20.8 %all_to_all.11 = f32[256,1,128]{2,1,0:T(1,128)S(1)} all-to-all(f32[256,1,128]{2,1,0:T(1,128)S(1)} %bitcast.9), channel_id=1, replica_groups=mesh['lon'=64,'lat'=4] {'lon','lat'}, dimensions={0} | all-to-all | bytes 262144 | tf_op jit(solution)/shard_map/all_to_all | solution.py:919
  65.5 1.6 %shard_map.82 = (f32[2,64,256]{2,1,0:T(8,128)}, f32[2,64,256]{2,1,0:T(8,128)}, f32[2,64,256]{2,1,0:T(8,128)}) custom-call(f32[256,128]{1,0:T(8,128)S(1)} %bitcast.7, f32[2,48,256]{2,1,0:T(8,128)S(1)} %get-tuple-element.52.own_part.early_part, f32[2,48,256]{2,1,0:T(8,128)S(1)} %get-tuple-element.61.later_part, f32[344,8,256]{2,1,0:T(8,128)S(1)} %get-tuple-element.62.basis), custom_call_target="tpu_custom_call" | custom-call | tf_op jit(solution)/shard_map/pallas_call | solution.py:921
  (3 shorter events, 0.0 us)
Async XLA Ops:
  2.3 11.6 %collective-permute-start = (f32[48,256]{1,0:T(8,128)S(1)}, f32[48,256]{1,0:T(8,128)S(1)}, u32[]{:S(2)}, u32[]{:S(2)}) collective-permute-start(f32[48,256]{1,0:T(8,128)S(1)} %get-tuple-element.39), channel_id=1, source_target_pairs={{0,252},{4,8},{8,4},{12,16},{16,12},{20,24},{24,20},{28,32},{32,28... | collective-permute-start | bytes 147464 | tf_op jit(solution)/shard_map/ppermute | solution.py:842
  12.0 2.9 %collective-permute-start.1 = (f32[48,256]{1,0:T(8,128)S(1)}, f32[48,256]{1,0:T(8,128)S(1)}, u32[]{:S(2)}, u32[]{:S(2)}) collective-permute-start(f32[48,256]{1,0:T(8,128)S(1)} %get-tuple-element.40), channel_id=1, source_target_pairs={{0,4},{4,0},{8,12},{12,8},{16,20},{20,16},{24,28},{28,24},{32,36},... | collective-permute-start | bytes 147464 | tf_op jit(solution)/shard_map/ppermute | solution.py:843
  29.2 7.2 %collective-permute-start.2 = (f32[24,128]{1,0:T(8,128)S(1)}, f32[24,128]{1,0:T(8,128)S(1)}, u32[]{:S(2)}, u32[]{:S(2)}) collective-permute-start(f32[24,128]{1,0:T(8,128)S(1)} %get-tuple-element.43), channel_id=1, source_target_pairs={{0,252},{4,8},{8,4},{12,16},{16,12},{20,24},{24,20},{28,32},{32,28... | collective-permute-start | bytes 36872 | tf_op jit(solution)/shard_map/ppermute | solution.py:894
  33.2 3.3 %collective-permute-start.3 = (f32[24,128]{1,0:T(8,128)S(1)}, f32[24,128]{1,0:T(8,128)S(1)}, u32[]{:S(2)}, u32[]{:S(2)}) collective-permute-start(f32[24,128]{1,0:T(8,128)S(1)} %get-tuple-element.45), channel_id=1, source_target_pairs={{0,4},{4,0},{8,12},{12,8},{16,20},{20,16},{24,28},{28,24},{32,36},... | collective-permute-start | bytes 36872 | tf_op jit(solution)/shard_map/ppermute | solution.py:895

commit v4 on v3

--- a/solution.py
+++ b/solution.py
@@ -32,7 +32,7 @@
     found = []
     for tile in range(ref.shape[0]):
         if stride == 0:
-            found.append(ref[tile, pl.ds(row, 8, stride=0), :])
+            found.append(jnp.broadcast_to(ref[tile, pl.ds(row, 1), :], (8, LANES)))
         else:
             found.append(ref[tile, pl.ds(row, 8, stride=stride), :])
     return jnp.concatenate(found, axis=1)
@@ -375,9 +375,8 @@
                 weight = same_row(jacobi.at[level], row, 0)
                 for word in range(2):
                     if own:
-                        place = pl.ds(row, 8, stride=0)
-                        part = jacobi[level, tiles - 1, place, :]
-                        held = word_bits[word, level, tiles - 1, place, :]
+                        part = row_of(jacobi.at[level, tiles - 1], row)
+                        held = row_of(word_bits.at[word, level, tiles - 1], row)
                         part = jnp.where((held & bit[:, :LANES]) != 0, part, -part)
                         fine = jnp.concatenate([begin[level, word, row - TOP], part], axis=1)
                     else:

time: 67.2 us -> 67.2 us (level)
  no operation moved by 1% of the time
where the time goes in v4:
time: 67.2 us; the launch traced here: 67.1 us
  blocking collectives  37.4 us (56%)
  Pallas kernels  14.3 us (21%)
  starting transfers between devices  13.7 us (20%)
  waiting for transfers between devices  1.02 us (2%)
  between operations  0.7 us (1%)
    all_to_all x1, blocking collectives, per_device(): everyone = lax.all_to_all(packed, ('lon', 'lat'), 0, 0)  20.8 us
    pallas_call x6, Pallas kernels, _run(): pl.pallas_call(kernel, out_shape=outs, in_specs=[pl.BlockSpec(memory_spac...  12.7 us
    ppermute x1, starting transfers between devices, per_device(): from_odd = lax.ppermute(to_odd, 'lon', odds)  9.7 us
    all_gather x1, blocking collectives, per_device(): gathered = lax.all_gather(merged, 'lat')  9.05 us
    all_gather x1, blocking collectives, per_device(): lax.all_gather(jnp.concatenate([sums_odd + own_sums[:24], sums_even + own...  7.53 us
    ppermute x1, starting transfers between devices, per_device(): sums_odd = lax.ppermute(to_odd, 'lon', odds)  3.98 us
    pallas_call x1, Pallas kernels, per_device(): pl.pallas_call(finish_kernel, out_shape=(shape(2, lon_rows, width),) * 3,...  1.56 us
  transfers between devices with their start and end apart: 4, of which 1 were waited for; matrix products, arithmetic and copies ran while one was open for 0% of the time, Pallas kernels for 8%

profile of v4, /device:TPU:1, one launch (start us, length us, event | category | flops | bytes accessed | tf_op | source)
XLA Modules:
  0.0 67.1 jit_solution(18035541481465678725)
XLA Ops:
  0.6 1.6 %shard_map.77 = (f32[48,256]{1,0:T(8,128)S(1)}, f32[48,256]{1,0:T(8,128)S(1)}, f32[96,128]{1,0:T(8,128)S(1)}, f32[2,48,256]{2,1,0:T(8,128)S(1)}) custom-call(f32[2,64,256]{2,1,0:T(8,128)} %obs_in.3, f32[2,64,256]{2,1,0:T(8,128)} %kap_in.3, s32[2,2,64,256]{3,2,1,0:T(8,128)} %bits_in.3, s32[64,256]{1,0:T(8,128)} %land_in.3), custom_call_target="tpu_custom_call" | custom-call | tf_op jit(solution)/shard_map/pallas_call | solution.py:812
  2.3 9.7 %collective-permute-start = (f32[48,256]{1,0:T(8,128)S(1)}, f32[48,256]{1,0:T(8,128)S(1)}, u32[]{:S(2)}, u32[]{:S(2)}) collective-permute-start(f32[48,256]{1,0:T(8,128)S(1)} %get-tuple-element.39), channel_id=1, source_target_pairs={{0,252},{4,8},{8,4},{12,16},{16,12},{20,24},{24,20},{28,32},{32,28... | collective-permute-start | bytes 147464 | tf_op jit(solution)/shard_map/ppermute | solution.py:841
  12.0 0.0 collective-permute-start.1
  12.0 1.9 %shard_map.76 = (f32[2,128,384]{2,1,0:T(8,128)S(1)}, f32[2,80,128]{2,1,0:T(8,128)S(1)}, f32[2,2,80,128]{3,2,1,0:T(8,128)S(1)}, f32[2,2,80,128]{3,2,1,0:T(8,128)S...) custom-call(f32[2,64,256]{2,1,0:T(8,128)} %obs_in.3, ...), custom_call_target="tpu_custom_call" | custom-call | tf_op jit(solution)/shard_map/pallas_call | solution.py:812
  13.9 0.0 collective-permute-done.from_odd
  13.9 1.0 %collective-permute-done.1.from_even = f32[48,256]{1,0:T(8,128)S(1)} collective-permute-done((f32[48,256]{1,0:T(8,128)S(1)}, f32[48,256]{1,0:T(8,128)S(1)}, u32[]{:S(2)}, u32[]{:S(2)}) %collective-permute-start.1) | collective-permute-done | bytes 49184 | tf_op jit(solution)/shard_map/ppermute | solution.py:842
  14.9 9.0 %all-gather = f32[384,128]{1,0:T(8,128)S(1)} all-gather(f32[96,128]{1,0:T(8,128)S(1)} %shard_map.78), channel_id=2, replica_groups=mesh['lon'=64,'lat'=4] {'lat'}, dimensions={0}, use_global_device_ids=true | all-gather | bytes 245760 | tf_op jit(solution)/shard_map/all_gather | solution.py:863
  24.0 5.2 %shard_map.79 = (f32[2,2,66,8,384]{4,3,2,1,0:T(8,128)S(1)}, f32[2,10,8,384]{3,2,1,0:T(8,128)S(1)}, f32[24,128]{1,0:T(8,128)S(1)}, f32[24,128]{1,0:T(8,128)S(1)},...) custom-call(f32[2,80,128]{2,1,0:T(8,128)S(1)} %get-tuple-element.33., ...), custom_call_target="tpu_custom_call" | custom-call | tf_op jit(solution)/shard_map/pallas_call | solution.py:812
  29.2 4.0 %collective-permute-start.2 = (f32[24,128]{1,0:T(8,128)S(1)}, f32[24,128]{1,0:T(8,128)S(1)}, u32[]{:S(2)}, u32[]{:S(2)}) collective-permute-start(f32[24,128]{1,0:T(8,128)S(1)} %get-tuple-element.43), channel_id=1, source_target_pairs={{0,252},{4,8},{8,4},{12,16},{16,12},{20,24},{24,20},{28,32},{32,28... | collective-permute-start | bytes 36872 | tf_op jit(solution)/shard_map/ppermute | solution.py:893
  33.2 0.0 collective-permute-start.3
  33.2 3.2 %shard_map.80 = (f32[2,2,3,4,8,256]{5,4,3,2,1,0:T(8,128)S(1)}, f32[2,2,16,256]{3,2,1,0:T(8,128)S(1)}, f32[4,2,3,8,256]{4,3,2,1,0:T(8,128)S(1)}, f32[4,8,256]{2,1...) custom-call(f32[2,2,66,8,384]{4,3,2,1,0:T(8,128)S(1)} %get-tuple-element.47.image, ...), custom_call_target="tpu_custom_call" | custom-call | tf_op jit(solution)/shard_map/pallas_call | solution.py:812
  36.4 0.0 collective-permute-done.2
  36.4 0.0 collective-permute-done.3
  36.5 7.5 %all-gather.1 = f32[192,128]{1,0:T(8,128)S(1)} all-gather(f32[48,128]{1,0:T(8,128)S(1)} %pad_maximum_fusion), channel_id=3, replica_groups=mesh['lon'=64,'lat'=4] {'lat'}, dimensions={0}, use_global_device_ids=true | all-gather | bytes 122880 | tf_op jit(solution)/shard_map/all_gather | solution.py:912
  44.0 0.7 %shard_map.81 = (f32[256,128]{1,0:T(8,128)S(1)}, f32[2,48,256]{2,1,0:T(8,128)S(1)}) custom-call(f32[4,48,128]{2,1,0:T(8,128)S(1)} %bitcast.8, f32[2,128,384]{2,1,0:T(8,128)S(1)} %get-tuple-element.42.spread, f32[2,48,256]{2,1,0:T(8,128)S(1)} %get-tuple-element.46.row_sums, f32[2,2,3,4,8,256]{5,4,3,2,1,0:T(8,128)S(1)} %get-tuple-element.54.linear, ...), custom_call_target="tpu_custom_call" | custom-call | tf_op jit(solution)/shard_map/pallas_call | solution.py:812
  44.7 20.8 %all_to_all.11 = f32[256,1,128]{2,1,0:T(1,128)S(1)} all-to-all(f32[256,1,128]{2,1,0:T(1,128)S(1)} %bitcast.9), channel_id=1, replica_groups=mesh['lon'=64,'lat'=4] {'lon','lat'}, dimensions={0} | all-to-all | bytes 262144 | tf_op jit(solution)/shard_map/all_to_all | solution.py:918
  65.5 1.6 %shard_map.82 = (f32[2,64,256]{2,1,0:T(8,128)}, f32[2,64,256]{2,1,0:T(8,128)}, f32[2,64,256]{2,1,0:T(8,128)}) custom-call(f32[256,128]{1,0:T(8,128)S(1)} %bitcast.7, f32[2,48,256]{2,1,0:T(8,128)S(1)} %get-tuple-element.52.own_part.early_part, f32[2,48,256]{2,1,0:T(8,128)S(1)} %get-tuple-element.61.later_part, f32[344,8,256]{2,1,0:T(8,128)S(1)} %get-tuple-element.62.basis), custom_call_target="tpu_custom_call" | custom-call | tf_op jit(solution)/shard_map/pallas_call | solution.py:920
  (3 shorter events, 0.0 us)
Async XLA Ops:
  2.3 11.6 %collective-permute-start = (f32[48,256]{1,0:T(8,128)S(1)}, f32[48,256]{1,0:T(8,128)S(1)}, u32[]{:S(2)}, u32[]{:S(2)}) collective-permute-start(f32[48,256]{1,0:T(8,128)S(1)} %get-tuple-element.39), channel_id=1, source_target_pairs={{0,252},{4,8},{8,4},{12,16},{16,12},{20,24},{24,20},{28,32},{32,28... | collective-permute-start | bytes 147464 | tf_op jit(solution)/shard_map/ppermute | solution.py:841
  12.0 2.9 %collective-permute-start.1 = (f32[48,256]{1,0:T(8,128)S(1)}, f32[48,256]{1,0:T(8,128)S(1)}, u32[]{:S(2)}, u32[]{:S(2)}) collective-permute-start(f32[48,256]{1,0:T(8,128)S(1)} %get-tuple-element.40), channel_id=1, source_target_pairs={{0,4},{4,0},{8,12},{12,8},{16,20},{20,16},{24,28},{28,24},{32,36},... | collective-permute-start | bytes 147464 | tf_op jit(solution)/shard_map/ppermute | solution.py:842
  29.2 7.2 %collective-permute-start.2 = (f32[24,128]{1,0:T(8,128)S(1)}, f32[24,128]{1,0:T(8,128)S(1)}, u32[]{:S(2)}, u32[]{:S(2)}) collective-permute-start(f32[24,128]{1,0:T(8,128)S(1)} %get-tuple-element.43), channel_id=1, source_target_pairs={{0,252},{4,8},{8,4},{12,16},{16,12},{20,24},{24,20},{28,32},{32,28... | collective-permute-start | bytes 36872 | tf_op jit(solution)/shard_map/ppermute | solution.py:893
  33.2 3.3 %collective-permute-start.3 = (f32[24,128]{1,0:T(8,128)S(1)}, f32[24,128]{1,0:T(8,128)S(1)}, u32[]{:S(2)}, u32[]{:S(2)}) collective-permute-start(f32[24,128]{1,0:T(8,128)S(1)} %get-tuple-element.45), channel_id=1, source_target_pairs={{0,4},{4,0},{8,12},{12,8},{16,20},{20,16},{24,28},{28,24},{32,36},... | collective-permute-start | bytes 36872 | tf_op jit(solution)/shard_map/ppermute | solution.py:894
